TPU v7x, 32 devices: a whole 2x2x4 slice. The times are simulated.
32 devices in a mesh: dp: 8 (over y, x, core), tensor: 4 (over z).
Axes of the slice: x: 2, y: 2, z: 4, core: 2. Of those that a mesh axis runs over, the one named last changes fastest.
Arguments:
- inputs: bfloat16 [16384, 2048], P(('dp', 'tensor')), may hold values from -51 to 51
- w_query: bfloat16 [2048, 2048], P('dp', 'tensor'), may hold values from -1 to 1
- w_key: bfloat16 [2048, 2048], P('dp', 'tensor'), may hold values from -1 to 1
- w_value: bfloat16 [2048, 2048], P('dp', 'tensor'), may hold values from -0.125 to 0.125
- w_out: bfloat16 [2048, 2048], P('tensor', 'dp'), may hold values from -1.5 to 1.5
- gain_one: bfloat16 [2048], P('dp'), may hold values from 0.5 to 1.5
- w_gate: bfloat16 [2048, 8192], P('dp', 'tensor'), may hold values from -0.125 to 0.125
- w_up: bfloat16 [2048, 8192], P('dp', 'tensor'), may hold values from -0.125 to 0.125
- w_down: bfloat16 [8192, 2048], P('tensor', 'dp'), may hold values from -0.0625 to 0.0625
- gain_two: bfloat16 [2048], P('dp'), may hold values from 0.5 to 1.5
- cotangent: bfloat16 [16384, 2048], P(('dp', 'tensor')), may hold values from -6 to 6
Outputs:
- output: bfloat16 [16384, 2048], P(('dp', 'tensor'))
- input_grad: float32 [16384, 2048], P(('dp', 'tensor'))
- grad_query: float32 [2048, 2048], P('dp', 'tensor')
- grad_key: float32 [2048, 2048], P('dp', 'tensor')
- grad_value: float32 [2048, 2048], P('dp', 'tensor')
- grad_out: float32 [2048, 2048], P('tensor', 'dp')
- grad_gain_one: float32 [2048], P(('dp', 'tensor'))
- grad_gate: float32 [2048, 8192], P('dp', 'tensor')
- grad_up: float32 [2048, 8192], P('dp', 'tensor')
- grad_down: float32 [8192, 2048], P('tensor', 'dp')
- grad_gain_two: float32 [2048], P(('dp', 'tensor'))
All inputs are finite; a program needn't handle non-finite values.
Results may differ from a plain program's by a relative error of at most 0.018.
Values may be sent and summed in bfloat16 or wider, within the bound.
No kernel may reach another device: no remote copies, remote signals or barrier semaphores. Data moves between devices by JAX's collectives and lax.ppermute only.
A program may use at most 184 MiB of HBM per device.

v0:
```python
import jax
import jax.numpy as jnp
from jax import lax
from jax.sharding import PartitionSpec as P

HD = 64
LEN = 1024


epsilon = 1e-05
rope_base = 130000.0


def rms_scale(matrix, gain):
    inverse = lax.rsqrt(jnp.mean(matrix * matrix, axis=-1, keepdims=True) + epsilon)
    return matrix * inverse * gain


def norm_back(matrix, gain, upstream):
    result, pull = jax.vjp(rms_scale, matrix, gain)
    return pull(upstream)


def rotate(tensor, positions, direction):
    half_size = tensor.shape[-1] // 2
    exponents = jnp.arange(half_size, dtype=jnp.float32) * (-2.0 / tensor.shape[-1])
    frequency = jnp.power(jnp.float32(rope_base), exponents)
    angles = positions.astype(jnp.float32)[:, None] * frequency[None, :]
    cosine = jnp.cos(angles)[:, None, :]
    sines = direction * jnp.sin(angles)[:, None, :]
    former = tensor[..., :half_size]
    latter = tensor[..., half_size:]
    return jnp.concatenate(
        [former * cosine - latter * sines, latter * cosine + former * sines], axis=-1
    )


def contract(left, right, left_dim, right_dim):
    return lax.dot_general(
        left, right, (((left_dim,), (right_dim,)), ((), ())), preferred_element_type=jnp.float32
    )


def block_scores(query_block, key_seq, offset, scaling):
    block_rows = query_block.shape[0]
    length = key_seq.shape[0]
    scores = (
        jnp.einsum("qhd,khd->hqk", query_block, key_seq, preferred_element_type=jnp.float32)
        * scaling
    )
    causal = (offset + jnp.arange(block_rows))[:, None] >= jnp.arange(length)[None, :]
    return jnp.where(causal[None], scores, -1e30)


def attend_forward(queries, key_rows, value_rows):
    sequences, length, head_count, head_size = queries.shape
    block_rows = min(512, length)
    blocks = length // block_rows
    scaling = head_size ** (-0.5)

    def attend_one_block(position_index):
        sequence = position_index // blocks
        offset = position_index % blocks * block_rows
        query_block = lax.dynamic_slice(
            queries, (sequence, offset, 0, 0), (1, block_rows, head_count, head_size)
        )[0]
        key_seq = lax.dynamic_index_in_dim(key_rows, sequence, 0, keepdims=False)
        value_seq = lax.dynamic_index_in_dim(value_rows, sequence, 0, keepdims=False)
        scores = block_scores(query_block, key_seq, offset, scaling)
        row_max = jnp.max(scores, axis=-1, keepdims=True)
        exponent = jnp.exp(scores - row_max)
        row_sum = jnp.sum(exponent, axis=-1, keepdims=True)
        probabilities = (exponent / row_sum).astype(jnp.bfloat16)
        result = jnp.einsum(
            "hqk,khd->qhd", probabilities, value_seq, preferred_element_type=jnp.float32
        ).astype(jnp.bfloat16)
        return (result, (row_max + jnp.log(row_sum))[..., 0])

    results, log_sums = lax.map(attend_one_block, jnp.arange(sequences * blocks))
    return (results.reshape(sequences * length, head_count * head_size), log_sums)


def attend_backward(queries, key_rows, value_rows, grad_attended, log_sums):
    sequences, length, head_count, head_size = queries.shape
    block_rows = min(512, length)
    blocks = length // block_rows
    scaling = head_size ** (-0.5)

    def per_sequence(sequence):
        query_seq = lax.dynamic_index_in_dim(queries, sequence, 0, keepdims=False)
        key_seq = lax.dynamic_index_in_dim(key_rows, sequence, 0, keepdims=False)
        value_seq = lax.dynamic_index_in_dim(value_rows, sequence, 0, keepdims=False)
        grad_seq = lax.dynamic_index_in_dim(grad_attended, sequence, 0, keepdims=False)

        def per_one_block(carried, step_index):
            key_grad, value_grad = carried
            offset = step_index * block_rows
            query_block = lax.dynamic_slice_in_dim(query_seq, offset, block_rows, 0)
            grad_block = lax.dynamic_slice_in_dim(grad_seq, offset, block_rows, 0)
            block_lse = lax.dynamic_index_in_dim(
                log_sums, sequence * blocks + step_index, 0, keepdims=False
            )
            scores = block_scores(query_block, key_seq, offset, scaling)
            probabilities = jnp.exp(scores - block_lse[..., None])
            rounded_probs = probabilities.astype(jnp.bfloat16)
            grad_probs = jnp.einsum(
                "qhd,khd->hqk", grad_block, value_seq, preferred_element_type=jnp.float32
            )
            row_dot = jnp.sum(probabilities * grad_probs, axis=-1, keepdims=True)
            grad_scores = (probabilities * (grad_probs - row_dot)).astype(jnp.bfloat16)
            query_grad = (
                jnp.einsum("hqk,khd->qhd", grad_scores, key_seq, preferred_element_type=jnp.float32)
                * scaling
            )
            key_grad = (
                key_grad
                + jnp.einsum(
                    "hqk,qhd->khd", grad_scores, query_block, preferred_element_type=jnp.float32
                )
                * scaling
            )
            value_grad = value_grad + jnp.einsum(
                "hqk,qhd->khd", rounded_probs, grad_block, preferred_element_type=jnp.float32
            )
            return ((key_grad, value_grad), query_grad)

        empty = jnp.zeros((length, head_count, head_size), jnp.float32)
        (key_grad, value_grad), query_grad = lax.scan(
            per_one_block, (empty, empty), jnp.arange(blocks)
        )
        return (query_grad.reshape(length, head_count, head_size), key_grad, value_grad)

    return lax.map(per_sequence, jnp.arange(sequences))


def on_device(
    inputs, w_query, w_key, w_value, w_out, gain_one, w_gate, w_up, w_down, gain_two, cotangent
):
    features = inputs.astype(jnp.float32)
    query_full, key_full, value_full, out_full, gain_first = (
        lax.all_gather(w_query, "dp", axis=0, tiled=True),
        lax.all_gather(w_key, "dp", axis=0, tiled=True),
        lax.all_gather(w_value, "dp", axis=0, tiled=True),
        lax.all_gather(w_out, "dp", axis=1, tiled=True),
        lax.all_gather(gain_one, "dp", axis=0, tiled=True),
    )
    gain_one_f = gain_first.astype(jnp.float32)
    normed_one = lax.all_gather(
        rms_scale(features, gain_one_f).astype(jnp.bfloat16), "tensor", axis=0, tiled=True
    )
    group_rows = normed_one.shape[0]
    sequences = group_rows // LEN
    head_count = w_query.shape[1] // HD
    positions = jnp.arange(group_rows) % LEN
    shaped = (sequences, LEN, head_count, HD)

    def project(weight):
        return jnp.dot(normed_one, weight, preferred_element_type=jnp.float32)

    queries = rotate(
        project(query_full).reshape(group_rows, head_count, HD), positions, 1.0
    ).astype(jnp.bfloat16)
    key_rows = rotate(project(key_full).reshape(group_rows, head_count, HD), positions, 1.0).astype(
        jnp.bfloat16
    )
    value_rows = project(value_full).astype(jnp.bfloat16)
    attended, log_sums = attend_forward(
        queries.reshape(shaped), key_rows.reshape(shaped), value_rows.reshape(shaped)
    )
    own_tokens = lax.all_to_all(attended, "tensor", split_axis=0, concat_axis=1, tiled=True)
    out_whole = lax.all_gather(out_full, "tensor", axis=0, tiled=True)
    hidden_state = features + jnp.dot(own_tokens, out_whole, preferred_element_type=jnp.float32)
    gate_full, up_full, down_full, gain_second = (
        lax.all_gather(w_gate, "dp", axis=0, tiled=True),
        lax.all_gather(w_up, "dp", axis=0, tiled=True),
        lax.all_gather(w_down, "dp", axis=1, tiled=True),
        lax.all_gather(gain_two, "dp", axis=0, tiled=True),
    )
    gain_two_f = gain_second.astype(jnp.float32)
    normed_two = lax.all_gather(
        rms_scale(hidden_state, gain_two_f).astype(jnp.bfloat16), "tensor", axis=0, tiled=True
    )
    gate_proj = jnp.dot(normed_two, gate_full, preferred_element_type=jnp.float32)
    up_proj = jnp.dot(normed_two, up_full, preferred_element_type=jnp.float32)
    inner = (jax.nn.silu(gate_proj) * up_proj).astype(jnp.bfloat16)
    output = (
        hidden_state
        + lax.psum_scatter(
            jnp.dot(inner, down_full, preferred_element_type=jnp.float32).astype(jnp.bfloat16),
            "tensor",
            scatter_dimension=0,
            tiled=True,
        ).astype(jnp.float32)
    ).astype(jnp.bfloat16)
    gate_back, up_back, down_back = (
        lax.all_gather(w_gate, "dp", axis=0, tiled=True),
        lax.all_gather(w_up, "dp", axis=0, tiled=True),
        lax.all_gather(w_down, "dp", axis=1, tiled=True),
    )
    cot_all = lax.all_gather(cotangent, "tensor", axis=0, tiled=True)
    d_inner = contract(cot_all, down_back, 1, 1)
    grad_down = contract(inner, cot_all, 0, 0)
    sigmoid_gate = jax.nn.sigmoid(gate_proj)
    d_gate = (d_inner * up_proj * sigmoid_gate * (1.0 + gate_proj * (1.0 - sigmoid_gate))).astype(
        jnp.bfloat16
    )
    d_up = (d_inner * (gate_proj * sigmoid_gate)).astype(jnp.bfloat16)
    grad_gate = contract(normed_two, d_gate, 0, 0)
    grad_up = contract(normed_two, d_up, 0, 0)
    d_normed_two = lax.psum_scatter(
        contract(d_gate, gate_back, 1, 1) + contract(d_up, up_back, 1, 1),
        "tensor",
        scatter_dimension=0,
        tiled=True,
    )
    hidden_grad, grad_gain_two = norm_back(hidden_state, gain_two_f, d_normed_two)
    d_hidden = cotangent.astype(jnp.float32) + hidden_grad
    query_back, key_back, value_back, out_back = (
        lax.all_gather(w_query, "dp", axis=0, tiled=True),
        lax.all_gather(w_key, "dp", axis=0, tiled=True),
        lax.all_gather(w_value, "dp", axis=0, tiled=True),
        lax.all_gather(w_out, "dp", axis=1, tiled=True),
    )
    mixed_all = lax.all_gather(d_hidden.astype(jnp.bfloat16), "tensor", axis=0, tiled=True)
    grad_out = contract(attended, mixed_all, 0, 0)
    d_attended = contract(mixed_all, out_back, 1, 1).astype(jnp.bfloat16)
    query_grad, key_grad, value_grad = attend_backward(
        queries.reshape(shaped),
        key_rows.reshape(shaped),
        value_rows.reshape(shaped),
        d_attended.reshape(shaped),
        log_sums,
    )
    d_query = (
        rotate(query_grad.reshape(group_rows, head_count, HD), positions, -1.0)
        .reshape(group_rows, head_count * HD)
        .astype(jnp.bfloat16)
    )
    d_key = (
        rotate(key_grad.reshape(group_rows, head_count, HD), positions, -1.0)
        .reshape(group_rows, head_count * HD)
        .astype(jnp.bfloat16)
    )
    d_value = value_grad.reshape(group_rows, head_count * HD).astype(jnp.bfloat16)
    grad_query = contract(normed_one, d_query, 0, 0)
    grad_key = contract(normed_one, d_key, 0, 0)
    grad_value = contract(normed_one, d_value, 0, 0)
    d_normed_one = lax.psum_scatter(
        (
            contract(d_query, query_back, 1, 1)
            + contract(d_key, key_back, 1, 1)
            + contract(d_value, value_back, 1, 1)
        ).astype(jnp.bfloat16),
        "tensor",
        scatter_dimension=0,
        tiled=True,
    ).astype(jnp.float32)
    feature_grad, grad_gain_one = norm_back(features, gain_one_f, d_normed_one)
    input_grad = d_hidden + feature_grad
    summed = (
        lax.psum_scatter(
            grad_query.astype(jnp.bfloat16), "dp", scatter_dimension=0, tiled=True
        ).astype(jnp.float32),
        lax.psum_scatter(
            grad_key.astype(jnp.bfloat16), "dp", scatter_dimension=0, tiled=True
        ).astype(jnp.float32),
        lax.psum_scatter(
            grad_value.astype(jnp.bfloat16), "dp", scatter_dimension=0, tiled=True
        ).astype(jnp.float32),
        lax.psum_scatter(
            grad_out.astype(jnp.bfloat16), "dp", scatter_dimension=1, tiled=True
        ).astype(jnp.float32),
        lax.psum_scatter(
            grad_gate.astype(jnp.bfloat16), "dp", scatter_dimension=0, tiled=True
        ).astype(jnp.float32),
        lax.psum_scatter(
            grad_up.astype(jnp.bfloat16), "dp", scatter_dimension=0, tiled=True
        ).astype(jnp.float32),
        lax.psum_scatter(
            grad_down.astype(jnp.bfloat16), "dp", scatter_dimension=1, tiled=True
        ).astype(jnp.float32),
    )
    gain_sums = (
        lax.psum_scatter(grad_gain_one, ("dp", "tensor"), scatter_dimension=0, tiled=True),
        lax.psum_scatter(grad_gain_two, ("dp", "tensor"), scatter_dimension=0, tiled=True),
    )
    return (
        output,
        input_grad,
        summed[0],
        summed[1],
        summed[2],
        summed[3],
        gain_sums[0],
        summed[4],
        summed[5],
        summed[6],
        gain_sums[1],
    )


def solution(mesh):
    return jax.shard_map(
        on_device,
        mesh=mesh,
        in_specs=(
            P(("dp", "tensor"), None),
            P("dp", "tensor"),
            P("dp", "tensor"),
            P("dp", "tensor"),
            P("tensor", "dp"),
            P("dp"),
            P("dp", "tensor"),
            P("dp", "tensor"),
            P("tensor", "dp"),
            P("dp"),
            P(("dp", "tensor"), None),
        ),
        out_specs=(
            P(("dp", "tensor"), None),
            P(("dp", "tensor"), None),
            P("dp", "tensor"),
            P("dp", "tensor"),
            P("dp", "tensor"),
            P("tensor", "dp"),
            P(("dp", "tensor")),
            P("dp", "tensor"),
            P("dp", "tensor"),
            P("tensor", "dp"),
            P(("dp", "tensor")),
        ),
        check_vma=False,
    )
```

profile of v0, /device:TPU:0, one launch (start us, length us, event | category | flops | bytes accessed | tf_op | source)
XLA Modules:
  0.0 2256.6 jit_solution(2288151973860219381)
XLA Ops:
  9.4 10.4 all-gather
  27.8 12.9 all-gather.23.cloned.1.call-done
  43.4 27.1 %all-gather.17.cloned.1.call-done = bf16[2048,512]{1,0:T(8,128)(2,1)} async-done(((bf16[256,512]{1,0:T(8,128)(2,1)}), bf16[2048,512]{1,0:T(8,128)(2,1)}) %all-gather.17.cloned.1.call-update) | async-done | bytes 2097168 | tf_op jit(solution)/shard_map/all_gather | solution.py:143
  70.4 151.8 %all-gather.15.cloned.1.call-done = bf16[2048,2048]{1,0:T(8,128)(2,1)} async-done(((bf16[512,2048]{1,0:T(8,128)(2,1)}), bf16[2048,2048]{1,0:T(8,128)(2,1)}) %all-gather.15.cloned.1.call-update) | async-done | bytes 8388624 | tf_op jit(solution)/shard_map/all_gather | solution.py:148
  222.2 8.5 convolution_convert_fusion.9
  239.7 10.2 all-gather.21.cloned.1.call-done
  249.9 10.6 fusion.50
  260.5 19.0 all-gather.19.cloned.1.call-done
  279.5 8.0 fusion.49
  307.4 74.2 %while.45 = (s32[]{:T(128)}, bf16[4,512,8,64]{1,3,2,0:T(8,128)(2,1)}, f32[4,8,512]{2,1,0:T(8,128)}, s32[4]{0:T(128)S(1)}, bf16[2,1024,8,64]{1,3,2,0:T(8,128)(2,1...) while((s32[]{:T(128)}, ...), condition=%wide.region_4.5_spmd, body=%wide.region_1.4_spmd.sunk | while | flops 1124856320 | bytes 64100296 | solution.py:79
  356.8 5.7 fusion.121
  375.2 5.7 fusion.121
  386.3 8.9 all-gather.1
  395.2 80.0 %all-to-all-done = bf16[4,512,512]{1,2,0:T(8,128)(2,1)} async-done(((bf16[4,512,512]{1,2,0:T(8,128)(2,1)}), bf16[4,512,512]{1,2,0:T(8,128)(2,1)}, u32[]{:S(2)}, u32[]{:S(2)}) %all-to-all-start) | async-done | bytes 2097184 | tf_op jit(solution)/shard_map/all_to_all | solution.py:170
  475.1 9.8 multiply_reduce_fusion.3
  490.8 38.7 %all-gather.31.cloned.1.call-done = bf16[2048,2048]{1,0:T(8,128)(2,1)} async-done(((bf16[256,2048]{1,0:T(8,128)(2,1)}), bf16[2048,2048]{1,0:T(8,128)(2,1)}) %all-gather.31.cloned.1.call-update) | async-done | bytes 8388624 | tf_op jit(solution)/shard_map/all_gather | solution.py:175
  529.5 151.8 %all-gather.27.cloned.1.call-done = bf16[2048,2048]{1,0:T(8,128)(2,1)} async-done(((bf16[512,2048]{1,0:T(8,128)(2,1)}), bf16[2048,2048]{1,0:T(8,128)(2,1)}) %all-gather.27.cloned.1.call-update) | async-done | bytes 8388624 | tf_op jit(solution)/shard_map/all_gather | solution.py:180
  681.2 24.2 %fusion.52 = f32[2048,2048]{1,0:T(8,128)} fusion(bf16[2048,2048]{1,0:T(8,128)(2,1)} %all-gather.27.cloned.1.call-done, bf16[2048,2048]{1,0:T(8,128)(2,1)} %all-gather.31.cloned.1.call-done), kind=kOutput, calls=%fused_computation.123 | convolution fusion | flops 17179869184 | bytes 33554432 | tf_op jit(solution)/shard_map/dot_general | solution.py:184
  705.5 30.1 %all-gather.29.cloned.1.call-done = bf16[2048,2048]{1,0:T(8,128)(2,1)} async-done(((bf16[256,2048]{1,0:T(8,128)(2,1)}), bf16[2048,2048]{1,0:T(8,128)(2,1)}) %all-gather.29.cloned.1.call-update) | async-done | bytes 8388624 | tf_op jit(solution)/shard_map/all_gather | solution.py:174
  735.6 24.2 %fusion.51 = f32[2048,2048]{1,0:T(8,128)} fusion(bf16[2048,2048]{1,0:T(8,128)(2,1)} %all-gather.27.cloned.1.call-done, bf16[2048,2048]{1,0:T(8,128)(2,1)} %all-gather.29.cloned.1.call-done), kind=kOutput, calls=%fused_computation.122 | convolution fusion | flops 17179869184 | bytes 33554432 | tf_op jit(solution)/shard_map/dot_general | solution.py:183
  759.8 126.9 %all-gather.35.cloned.1.call-done = bf16[2048,2048]{1,0:T(8,128)(2,1)} async-done(((bf16[512,2048]{1,0:T(8,128)(2,1)}), bf16[2048,2048]{1,0:T(8,128)(2,1)}) %all-gather.35.cloned.1.call-update) | async-done | bytes 8388624 | tf_op jit(solution)/shard_map/all_gather | solution.py:200
  886.7 56.0 %all-gather.33.cloned.1.call-done = bf16[2048,2048]{1,0:T(8,128)(2,1)} async-done(((bf16[2048,256]{1,0:T(8,128)(2,1)}), bf16[2048,2048]{1,0:T(8,128)(2,1)}) %all-gather.33.cloned.1.call-update) | async-done | bytes 8388624 | tf_op jit(solution)/shard_map/all_gather | solution.py:176
  942.6 36.8 %multiply_convert_fusion.1 = (bf16[2048,2048]{1,0:T(8,128)(2,1)}, bf16[2048,2048]{1,0:T(8,128)(2,1)}, bf16[2048,2048]{1,0:T(8,128)(2,1)}) fusion(f32[2048,2048]{1,0:T(8,128)} %fusion.51, f32[2048,2048]{1,0:T(8,128)} %fusion.52, bf16[2048,2048]{1,0:T(8,128)(2,1)} %all-gather.35.cloned.1.call-done, bf16[2048,2048]{1,0:T(8,128)(2,1)} %all-gather.33.cloned.1.call-done), kind=kOutput, calls=%fused_computation.52 | convolution fusion | flops 17242783744 | bytes 75497472 | tf_op jit(solution)/shard_map/dot_general | solution.py:39
  979.4 24.3 %fusion.53 = f32[2048,2048]{1,0:T(8,128)} fusion(bf16[2048,2048]{1,0:T(8,128)(2,1)} %get-tuple-element.450, bf16[2048,2048]{1,0:T(8,128)(2,1)} %all-gather.29.cloned.1.call-done), kind=kOutput, calls=%fused_computation.124 | convolution fusion | flops 17179869184 | bytes 33554432 | tf_op jit(solution)/shard_map/dot_general | solution.py:39
  1003.8 26.7 %convolution_add_fusion = f32[2048,2048]{1,0:T(8,128)} fusion(f32[2048,2048]{1,0:T(8,128)} %fusion.53, bf16[2048,2048]{1,0:T(8,128)(2,1)} %get-tuple-element.449, bf16[2048,2048]{1,0:T(8,128)(2,1)} %all-gather.31.cloned.1.call-done), kind=kOutput, calls=%fused_computation.57 | convolution fusion | flops 17184063488 | bytes 50331648 | tf_op jit(solution)/shard_map/dot_general | solution.py:39
  1030.5 280.5 %reduce-scatter.13.cloned.1.call-done = f32[512,2048]{1,0:T(8,128)} async-done(((f32[2048,2048]{1,0:T(8,128)}), f32[512,2048]{1,0:T(8,128)}) %reduce-scatter.13.cloned.1.call-update) | async-done | bytes 4194320 | tf_op jit(solution)/shard_map/reduce_scatter | solution.py:210
  1319.6 23.8 %convolution_convert_fusion = bf16[2048,2048]{1,0:T(8,128)(2,1)} fusion(bf16[2048,2048]{1,0:T(8,128)(2,1)} %get-tuple-element.451, bf16[2048,2048]{1,0:T(8,128)(2,1)} %all-gather.35.cloned.1.call-done), kind=kOutput, calls=%fused_computation.63 | convolution fusion | flops 17184063488 | bytes 25165824 | tf_op jit(solution)/shard_map/dot_general | solution.py:39
  1343.5 24.0 %convolution_convert_fusion.1 = bf16[2048,2048]{1,0:T(8,128)(2,1)} fusion(bf16[2048,2048]{1,0:T(8,128)(2,1)} %all-gather.27.cloned.1.call-done, bf16[2048,2048]{1,0:T(8,128)(2,1)} %get-tuple-element.449), kind=kOutput, calls=%fused_computation.64 | convolution fusion | flops 17184063488 | bytes 25165824 | tf_op jit(solution)/shard_map/dot_general | solution.py:39
  1367.5 23.9 %convolution_convert_fusion.2 = bf16[2048,2048]{1,0:T(8,128)(2,1)} fusion(bf16[2048,2048]{1,0:T(8,128)(2,1)} %all-gather.27.cloned.1.call-done, bf16[2048,2048]{1,0:T(8,128)(2,1)} %get-tuple-element.450), kind=kOutput, calls=%fused_computation.65 | convolution fusion | flops 17184063488 | bytes 25165824 | tf_op jit(solution)/shard_map/dot_general | solution.py:39
  1396.6 73.4 %all-gather.37.cloned.1.call-done = bf16[2048,2048]{1,0:T(8,128)(2,1)} async-done(((bf16[512,2048]{1,0:T(8,128)(2,1)}), bf16[2048,2048]{1,0:T(8,128)(2,1)}) %all-gather.37.cloned.1.call-update) | async-done | bytes 8388624 | tf_op jit(solution)/shard_map/all_gather | solution.py:224
  1469.9 8.6 convolution_convert_fusion.8
  1487.1 10.1 convolution_convert_fusion.4
  1497.2 301.2 %while.47 = (s32[]{:T(128)}, f32[2,1024,8,64]{3,2,1,0:T(8,128)}, f32[2,1024,8,64]{1,0,3,2:T(2,128)}, bf16[2,1024,8,64]{1,3,2,0:T(8,128)(2,1)}, s32[2]{0:T(128)S(...) while((s32[]{:T(128)}, f32[2,1024,8,64]{3,2,1,0:T(8,128)}, ...), condition=%wide.region_13.14_spmd, body=%wide.region_9.13_spmd.sunk | while | flops 2725507584 | bytes 273765440 | solution.py:133
  1506.7 92.6 %while.48 = (s32[]{:T(128)}, f32[1024,8,64]{0,2,1:T(8,128)}, f32[1024,8,64]{0,2,1:T(8,128)}, f32[2,512,8,64]{1,3,2,0:T(8,128)}, s32[2]{0:T(128)S(1)}, /*index=5*...) while((s32[]{:T(128)}, f32[1024,8,64]{0,2,1:T(8,128)}, ...), condition=%wide.region_12.12_spmd.clone, body=%wide.region_10.11_spmd.clone.sunk | while | flops 2725507584 | bytes 217141744 | solution.py:128
  1515.0 11.5 multiply_reduce_fusion.5
  1526.5 10.1 multiply_convert_fusion.6
  1536.7 9.0 bitcast_add_fusion.5
  1561.0 11.8 multiply_reduce_fusion.5
  1572.8 9.6 multiply_convert_fusion.6
  1582.4 10.0 bitcast_add_fusion.5
  1603.0 36.7 %dynamic_update_slice.46 = f32[2,1024,8,64]{1,0,3,2:T(2,128)} dynamic-update-slice(f32[2,1024,8,64]{1,0,3,2:T(2,128)} %get-tuple-element.798, f32[1,1024,8,64]{1,0,3,2:T(1,128)S(1)} %copy.82, s32[]{:T(128)S(6)} %copy.114, s32[]{:T(128)} %constant.187.clone.1..sunk.1, s32[]{:T(128)} %constant.187.clone.1..sunk.1, s32[]{:T(128)} %constant.187.clone.1..sunk.1) | dynamic-update-slice | bytes 4194308 | tf_op jit(solution)/shard_map/while/body/jit(dynamic_update_index_in_dim)/dynamic_update_slice | solution.py:133
  1658.3 90.5 %while.48 = (s32[]{:T(128)}, f32[1024,8,64]{0,2,1:T(8,128)}, f32[1024,8,64]{0,2,1:T(8,128)}, f32[2,512,8,64]{1,3,2,0:T(8,128)}, s32[2]{0:T(128)S(1)}, /*index=5*...) while((s32[]{:T(128)}, f32[1024,8,64]{0,2,1:T(8,128)}, ...), condition=%wide.region_12.12_spmd.clone, body=%wide.region_10.11_spmd.clone.sunk | while | flops 2725507584 | bytes 217141744 | solution.py:128
  1666.4 11.5 multiply_reduce_fusion.5
  1677.9 9.5 multiply_convert_fusion.6
  1687.5 9.0 bitcast_add_fusion.5
  1711.5 11.5 multiply_reduce_fusion.5
  1723.0 9.5 multiply_convert_fusion.6
  1732.4 9.6 bitcast_add_fusion.5
  1752.5 36.6 %dynamic_update_slice.46 = f32[2,1024,8,64]{1,0,3,2:T(2,128)} dynamic-update-slice(f32[2,1024,8,64]{1,0,3,2:T(2,128)} %get-tuple-element.798, f32[1,1024,8,64]{1,0,3,2:T(1,128)S(1)} %copy.82, s32[]{:T(128)S(6)} %copy.114, s32[]{:T(128)} %constant.187.clone.1..sunk.1, s32[]{:T(128)} %constant.187.clone.1..sunk.1, s32[]{:T(128)} %constant.187.clone.1..sunk.1) | dynamic-update-slice | bytes 4194308 | tf_op jit(solution)/shard_map/while/body/jit(dynamic_update_index_in_dim)/dynamic_update_slice | solution.py:133
  1803.0 6.4 convolution_convert_fusion.5
  1809.5 13.2 fusion.48
  1822.7 6.6 reshape.279
  1829.3 6.5 copy.70
  1835.7 6.4 copy.69
  1850.2 9.5 convolution_convert_fusion.6
  1860.2 9.9 convolution_convert_fusion.7
  1870.2 13.0 fusion.54
  1883.2 8.2 fusion.55
  1891.4 17.3 add_convert_fusion
  1909.0 24.0 %convolution_convert_fusion.3 = bf16[2048,2048]{1,0:T(8,128)(2,1)} fusion(bf16[2048,2048]{1,0:T(8,128)(2,1)} %get-tuple-element.451, bf16[2048,2048]{1,0:T(8,128)(2,1)} %all-gather.33.cloned.1.call-done), kind=kOutput, calls=%fused_computation.66 | convolution fusion | flops 17184063488 | bytes 25165824 | tf_op jit(solution)/shard_map/dot_general | solution.py:189
  1948.9 143.9 %reduce-scatter.15.cloned.1.call-done = bf16[512,2048]{1,0:T(8,128)(2,1)} async-done(((bf16[2048,2048]{1,0:T(8,128)(2,1)}), bf16[512,2048]{1,0:T(8,128)(2,1)}) %reduce-scatter.15.cloned.1.call-update) | async-done | bytes 2097168 | tf_op jit(solution)/shard_map/reduce_scatter | solution.py:248
  2096.1 46.2 %all-reduce.2 = (f32[2048]{0:T(1024)S(1)}, f32[2048]{0:T(1024)S(1)}) all-reduce(f32[2048]{0:T(1024)S(1)} %get-tuple-element.381, f32[2048]{0:T(1024)S(1)} %copy-done.35), channel_id=9, replica_groups=mesh['dp'=8,'tensor'=4] {'dp','tensor'}, use_global_device_ids=true, to_apply=%region_21.22.clone | all-reduce | flops 4096 | bytes 32768
  2143.5 97.8 %reduce-scatter.11.cloned.1.call-done = bf16[512,2048]{1,0:T(8,128)(2,1)} async-done(((bf16[2048,2048]{1,0:T(8,128)(2,1)}), bf16[512,2048]{1,0:T(8,128)(2,1)}) %reduce-scatter.11.cloned.1.call-update) | async-done | bytes 2097168 | tf_op jit(solution)/shard_map/reduce_scatter | solution.py:188
  2241.3 8.2 fusion.38
  (333 shorter events, 253.8 us)
Async XLA Ops:
  7.2 33.5 %all-gather.23.cloned.1.call-start = ((), (), s32[]{:S(2)}) async-start(), calls=%async_computation.15 | async-start | bytes 2359296 | tf_op jit(solution)/shard_map/all_gather | solution.py:144
  7.9 62.5 %all-gather.17.cloned.1.call-start = ((), (), s32[]{:S(2)}) async-start(), calls=%async_computation.12 | async-start | bytes 2359296 | tf_op jit(solution)/shard_map/all_gather | solution.py:143
  8.7 213.5 %all-gather.15.cloned.1.call-start = ((), (), s32[]{:S(2)}) async-start(), calls=%async_computation.11 | async-start | bytes 10485760 | tf_op jit(solution)/shard_map/all_gather | solution.py:148
  26.6 223.4 %all-gather.21.cloned.1.call-start = ((), (), s32[]{:S(2)}) async-start(), calls=%async_computation.14 | async-start | bytes 2359296 | tf_op jit(solution)/shard_map/all_gather | solution.py:142
  27.2 252.3 %all-gather.19.cloned.1.call-start = ((), (), s32[]{:S(2)}) async-start(), calls=%async_computation.13 | async-start | bytes 2359296 | tf_op jit(solution)/shard_map/all_gather | solution.py:141
  27.8 447.4 %all-gather.25.cloned.1.call-start = ((), (), s32[]{:S(2)}) async-start(), calls=%async_computation.16 | async-start | bytes 10485760 | tf_op jit(solution)/shard_map/all_gather | solution.py:171
  40.7 488.7 %all-gather.31.cloned.1.call-start = ((), (), s32[]{:S(2)}) async-start(), calls=%async_computation.19 | async-start | bytes 9437184 | tf_op jit(solution)/shard_map/all_gather | solution.py:175
  43.4 244.1 %copy-start.19 = (f32[2048,32]{0,1:T(8,128)}, f32[2048,32]{0,1:T(8,128)S(1)}, u32[]{:S(2)}) copy-start(f32[2048,32]{0,1:T(8,128)S(1)} %get-tuple-element.470) | copy-start | bytes 786436
  279.5 8.0 copy-start.18
  279.5 8.0 copy-start.24
  381.5 103.4 %copy-start.6 = (bf16[2,1024,8,64]{1,3,2,0:T(8,128)(2,1)}, bf16[2,1024,8,64]{1,3,2,0:T(8,128)(2,1)S(1)}, u32[]{:S(2)}) copy-start(bf16[2,1024,8,64]{1,3,2,0:T(8,128)(2,1)S(1)} %get-tuple-element.854) | copy-start | bytes 6291460
  381.5 93.6 %all-to-all-start = ((bf16[4,512,512]{1,2,0:T(8,128)(2,1)}), bf16[4,512,512]{1,2,0:T(8,128)(2,1)}, u32[]{:S(2)}, u32[]{:S(2)}) async-start(bf16[4,512,512]{1,2,0:T(8,128)(2,1)} %bitcast.177), calls=%async_computation | async-start | bytes 4194304 | tf_op jit(solution)/shard_map/all_to_all | solution.py:170
  386.2 295.0 %all-gather.27.cloned.1.call-start = ((), (), s32[]{:S(2)}) async-start(), calls=%async_computation.17 | async-start | bytes 10485760 | tf_op jit(solution)/shard_map/all_gather | solution.py:180
  395.2 90.3 %copy-start.25 = (f32[8,1,256]{2,1,0:T(1,128)}, f32[8,1,256]{2,1,0:T(1,128)S(1)}, u32[]{:S(2)}) copy-start(f32[8,1,256]{2,1,0:T(1,128)S(1)} %convert_element_type.213) | copy-start | bytes 24580
  488.7 246.9 %all-gather.29.cloned.1.call-start = ((), (), s32[]{:S(2)}) async-start(), calls=%async_computation.18 | async-start | bytes 9437184 | tf_op jit(solution)/shard_map/all_gather | solution.py:174
  489.4 397.2 %all-gather.35.cloned.1.call-start = ((), (), s32[]{:S(2)}) async-start(), calls=%async_computation.22 | async-start | bytes 10485760 | tf_op jit(solution)/shard_map/all_gather | solution.py:200
  490.0 452.6 %all-gather.33.cloned.1.call-start = ((), (), s32[]{:S(2)}) async-start(), calls=%async_computation.20 | async-start | bytes 9437184 | tf_op jit(solution)/shard_map/all_gather | solution.py:176
  490.8 820.3 %reduce-scatter.13.cloned.1.call-start = ((), (), s32[]{:S(2)}) async-start(), calls=%async_computation.23 | async-start | bytes 20971520 | tf_op jit(solution)/shard_map/reduce_scatter | solution.py:210
  1030.4 280.6 %copy-start.26 = (f32[8,1,256]{2,1,0:T(1,128)S(1)}, f32[8,1,256]{2,1,0:T(1,128)}, u32[]{:S(2)}) copy-start(f32[8,1,256]{2,1,0:T(1,128)} %copy-done.25) | copy-start | bytes 24580
  1030.4 280.6 %copy-start.31 = (f32[512]{0:T(512)S(1)}, f32[512]{0:T(512)}, u32[]{:S(2)}) copy-start(f32[512]{0:T(512)} %copy-done.30) | copy-start | bytes 6148
  1030.4 286.5 %copy-start.16 = (bf16[512,2048]{1,0:T(8,128)(2,1)S(1)}, bf16[512,2048]{1,0:T(8,128)(2,1)}, u32[]{:S(2)}) copy-start(bf16[512,2048]{1,0:T(8,128)(2,1)} %param.27) | copy-start | bytes 6291460
  1030.5 285.8 %copy-start.41 = (f32[512]{0:T(512)S(1)}, f32[512]{0:T(512)}, u32[]{:S(2)}) copy-start(f32[512]{0:T(512)} %copy-done.40) | copy-start | bytes 6148
  1030.5 439.5 %all-gather.37.cloned.1.call-start = ((), (), s32[]{:S(2)}) async-start(), calls=%async_computation.24 | async-start | bytes 10485760 | tf_op jit(solution)/shard_map/all_gather | solution.py:224
  1319.6 613.5 %reduce-scatter.29.cloned.1.call-start = ((), (), s32[]{:S(2)}) async-start(), calls=%async_computation.32 | async-start | bytes 9437184 | tf_op jit(solution)/shard_map/reduce_scatter | solution.py:279
  1343.4 592.4 %reduce-scatter.27.cloned.1.call-start = ((), (), s32[]{:S(2)}) async-start(), calls=%async_computation.31 | async-start | bytes 9437184 | tf_op jit(solution)/shard_map/reduce_scatter | solution.py:276
  1367.5 571.3 %reduce-scatter.25.cloned.1.call-start = ((), (), s32[]{:S(2)}) async-start(), calls=%async_computation.30 | async-start | bytes 9437184 | tf_op jit(solution)/shard_map/reduce_scatter | solution.py:273
  1391.4 550.2 %reduce-scatter.23.cloned.1.call-start = ((), (), s32[]{:S(2)}) async-start(), calls=%async_computation.29 | async-start | bytes 2359296 | tf_op jit(solution)/shard_map/reduce_scatter | solution.py:270
  1497.2 446.3 %reduce-scatter.21.cloned.1.call-start = ((), (), s32[]{:S(2)}) async-start(), calls=%async_computation.28 | async-start | bytes 2359296 | tf_op jit(solution)/shard_map/reduce_scatter | solution.py:267
  1497.7 9.0 copy-start.14
  1497.7 9.0 copy-start.45
  1526.5 10.1 copy-start.3
  1536.7 9.0 copy-start
  1536.7 9.8 copy-start.1
  1536.7 10.0 copy-start.4
  1572.8 9.6 copy-start.3
  1582.3 10.0 copy-start
  1582.3 10.6 copy-start.1
  1582.4 11.0 copy-start.4
  1649.0 9.2 copy-start.14
  1649.0 9.2 copy-start.45
  1677.9 9.5 copy-start.3
  1687.5 9.0 copy-start
  1687.5 9.5 copy-start.1
  1687.5 9.9 copy-start.4
  1723.0 9.5 copy-start.3
  1732.4 9.6 copy-start
  1732.4 9.8 copy-start.1
  1732.4 10.4 copy-start.4
  1809.4 135.8 %reduce-scatter.19.cloned.1.call-start = ((), (), s32[]{:S(2)}) async-start(), calls=%async_computation.27 | async-start | bytes 2359296 | tf_op jit(solution)/shard_map/reduce_scatter | solution.py:264
  1835.7 6.4 copy-start.20
  1835.7 6.4 copy-start.23
  1859.8 87.3 %reduce-scatter.17.cloned.1.call-start = ((), (), s32[]{:S(2)}) async-start(), calls=%async_computation.26 | async-start | bytes 2359296 | tf_op jit(solution)/shard_map/reduce_scatter | solution.py:261
  1870.1 222.7 %reduce-scatter.15.cloned.1.call-start = ((), (), s32[]{:S(2)}) async-start(), calls=%async_computation.25 | async-start | bytes 10485760 | tf_op jit(solution)/shard_map/reduce_scatter | solution.py:248
  1870.2 13.1 copy-start.22
  1870.2 13.1 copy-start.43
  1908.8 332.6 %reduce-scatter.11.cloned.1.call-start = ((), (), s32[]{:S(2)}) async-start(), calls=%async_computation.21 | async-start | bytes 10485760 | tf_op jit(solution)/shard_map/reduce_scatter | solution.py:188
  1935.8 157.0 %copy-start.12 = (bf16[512,2048]{1,0:T(8,128)(2,1)S(1)}, bf16[512,2048]{1,0:T(8,128)(2,1)}, u32[]{:S(2)}) copy-start(bf16[512,2048]{1,0:T(8,128)(2,1)} %param.17) | copy-start | bytes 6291460
  1935.8 157.0 %copy-start.29 = (f32[8,1,256]{2,1,0:T(1,128)S(1)}, f32[8,1,256]{2,1,0:T(1,128)}, u32[]{:S(2)}) copy-start(f32[8,1,256]{2,1,0:T(1,128)} %copy-done.28) | copy-start | bytes 24580
  1935.8 157.0 %copy-start.34 = (f32[512]{0:T(512)S(1)}, f32[512]{0:T(512)}, u32[]{:S(2)}) copy-start(f32[512]{0:T(512)} %copy-done.33) | copy-start | bytes 6148
  1941.6 154.5 %copy-start.35 = (f32[2048]{0:T(1024)S(1)}, f32[2048]{0:T(1024)}, u32[]{:S(2)}) copy-start(f32[2048]{0:T(1024)} %get-tuple-element.379) | copy-start | bytes 24580
  1941.6 201.9 %copy-start.39 = (f32[512]{0:T(512)S(1)}, f32[512]{0:T(512)}, u32[]{:S(2)}) copy-start(f32[512]{0:T(512)} %copy-done.38) | copy-start | bytes 6148
  1941.6 299.7 %copy-start.27 = (f32[8,1,256]{2,1,0:T(1,128)S(1)}, f32[8,1,256]{2,1,0:T(1,128)}, u32[]{:S(2)}) copy-start(f32[8,1,256]{2,1,0:T(1,128)} %copy-done.25) | copy-start | bytes 24580
  1941.6 299.7 %copy-start.32 = (f32[512]{0:T(512)S(1)}, f32[512]{0:T(512)}, u32[]{:S(2)}) copy-start(f32[512]{0:T(512)} %copy-done.30) | copy-start | bytes 6148
  1941.6 299.7 %copy-start.37 = (f32[512]{0:T(512)S(1)}, f32[512]{0:T(512)}, u32[]{:S(2)}) copy-start(f32[512]{0:T(512)} %copy-done.36) | copy-start | bytes 6148
  (35 other events, 89.4 us)
Sparse Core Ops, SparseCore 0:
  9.9 30.8 all-gather.22
  42.6 27.7 all-gather.16
  72.6 149.5 all-gather.14
  224.0 25.9 all-gather.20
  251.7 27.7 all-gather.18
  280.9 194.1 all-gather.24
  477.0 52.4 all-gather.30
  531.6 149.5 all-gather.26
  683.1 52.4 all-gather.28
  737.0 149.5 all-gather.34
  888.5 54.0 all-gather.32
  1030.6 280.4 reduce-scatter.12
  1319.7 150.2 all-gather.36
  1473.2 69.4 reduce-scatter.28
  1546.1 71.4 reduce-scatter.26
  1620.9 71.4 reduce-scatter.24
  1695.5 41.1 reduce-scatter.22
  1809.6 41.3 reduce-scatter.20
  1859.9 41.0 reduce-scatter.18
  1904.7 41.0 reduce-scatter.16
  1948.2 144.5 reduce-scatter.14
  2095.2 146.1 reduce-scatter.10
where the time goes:
time: 2270 us; the launch traced here: 2260 us
  waiting for transfers between devices  1310 us (58%)
  matrix products  508 us (22%)
  local copies, waits for them, and re-layouts  207 us (9%)
  other arithmetic  126 us (6%)
  blocking collectives  65.5 us (3%)
    reduce_scatter x1, waiting for transfers between devices, on_device(): lax.psum_scatter(contract(d_gate, gate_back, 1, 1) + contract(d_up, up_ba...  281 us
    dot_general x14, matrix products, contract(): lax.dot_general(left, right, (((left_dim,), (right_dim,)), ((), ())), pre...  242 us
    all_gather x1, waiting for transfers between devices, on_device(): lax.all_gather(rms_scale(features, gain_one_f).astype(jnp.bfloat16), 'ten...  152 us
    all_gather x1, waiting for transfers between devices, on_device(): lax.all_gather(rms_scale(hidden_state, gain_two_f).astype(jnp.bfloat16),...  152 us
    reduce_scatter x1, waiting for transfers between devices, on_device(): lax.psum_scatter((contract(d_query, query_back, 1, 1) + contract(d_key, k...  144 us
    all_gather x1, waiting for transfers between devices, on_device(): cot_all = lax.all_gather(cotangent, 'tensor', axis=0, tiled=True)  127 us
    reduce_scatter x1, waiting for transfers between devices, on_device(): lax.psum_scatter(jnp.dot(inner, down_full, preferred_element_type=jnp.flo...  97.8 us
    dynamic_update_slice x8, local copies, waits for them, and re-layouts, attend_backward(): return lax.map(per_sequence, jnp.arange(sequences))  91.1 us
  transfers between devices with their start and end apart: 23, of which 15 were waited for; matrix products, arithmetic and copies ran while one was open for 32% of the time, Pallas kernels for 0%

commit v1 on v0

v1 whole, which is shorter than its diff:
```python
import jax
import jax.numpy as jnp
from jax import lax
from jax.experimental import pallas as pl
from jax.experimental.pallas import tpu as pltpu
from jax.sharding import PartitionSpec as P

HD = 64
LEN = 1024
LANES = 128
Q_ROWS = 256
HID_TILE = 256
VMEM_BYTES = 60 * 1024 * 1024

epsilon = 1e-05
rope_base = 130000.0

f32 = jnp.float32
bf16 = jnp.bfloat16


def rms_scale(matrix, gain):
    inverse = lax.rsqrt(jnp.mean(matrix * matrix, axis=-1, keepdims=True) + epsilon)
    return matrix * inverse * gain


def norm_back(matrix, gain, upstream):
    result, pull = jax.vjp(rms_scale, matrix, gain)
    return pull(upstream)


def contract(left, right, left_dim, right_dim):
    return lax.dot_general(
        left, right, (((left_dim,), (right_dim,)), ((), ())), preferred_element_type=f32
    )


def rope_tables():
    half = HD // 2
    exponents = jnp.arange(half, dtype=f32) * (-2.0 / HD)
    frequency = jnp.power(f32(rope_base), exponents)
    angles = jnp.arange(LEN).astype(f32)[:, None] * frequency[None, :]
    cosine, sine = jnp.cos(angles), jnp.sin(angles)
    reps = LANES // HD
    return (
        jnp.concatenate([cosine, cosine] * reps, axis=1),
        jnp.concatenate([-sine, sine] * reps, axis=1),
    )


def turn(values, cosine, sine):
    lane = lax.broadcasted_iota(jnp.int32, values.shape, 1)
    other = jnp.where(
        lane % HD < HD // 2,
        pltpu.roll(values, LANES - HD // 2, 1),
        pltpu.roll(values, HD // 2, 1),
    )
    return values * cosine + other * sine


def project_kernel(x_ref, w_ref, cos_ref, sin_ref, out_ref):
    product = jnp.dot(x_ref[...], w_ref[...], preferred_element_type=f32)
    cosine, sine = cos_ref[...], sin_ref[...]
    out_ref[:, :LANES] = turn(product[:, :LANES], cosine, sine).astype(bf16)
    out_ref[:, LANES : 2 * LANES] = turn(product[:, LANES : 2 * LANES], cosine, sine).astype(bf16)
    out_ref[:, 2 * LANES :] = product[:, 2 * LANES :].astype(bf16)


def project(tokens, weights, columns, cosine, sine):
    rows, width = tokens.shape
    tile = 3 * LANES
    tile_rows = 512
    return pl.pallas_call(
        project_kernel,
        grid=(rows // tile_rows, columns // tile),
        in_specs=[
            pl.BlockSpec((tile_rows, width), lambda m, n: (m, 0)),
            pl.BlockSpec((width, tile), lambda m, n: (0, n)),
            pl.BlockSpec((tile_rows, LANES), lambda m, n: (m, 0)),
            pl.BlockSpec((tile_rows, LANES), lambda m, n: (m, 0)),
        ],
        out_specs=pl.BlockSpec((tile_rows, tile), lambda m, n: (m, n)),
        out_shape=jax.ShapeDtypeStruct((rows, columns), bf16),
        compiler_params=pltpu.CompilerParams(vmem_limit_bytes=VMEM_BYTES),
        cost_estimate=pl.CostEstimate(
            flops=2 * rows * width * columns,
            bytes_accessed=2 * (rows * width + width * columns + rows * columns),
            transcendentals=0,
        ),
        name="project",
    )(tokens, weights, cosine, sine)


def head_mask(shape, head):
    lane = lax.broadcasted_iota(jnp.int32, shape, 1)
    return lane // HD == head


def attend_kernel(qkv_ref, out_ref):
    length = qkv_ref.shape[0]
    scale = HD ** (-0.5)
    for block in range(length // Q_ROWS):
        low, high = block * Q_ROWS, (block + 1) * Q_ROWS
        total = jnp.zeros((Q_ROWS, LANES), f32)
        row = low + lax.broadcasted_iota(jnp.int32, (Q_ROWS, high), 0)
        col = lax.broadcasted_iota(jnp.int32, (Q_ROWS, high), 1)
        for head in range(LANES // HD):
            query = qkv_ref[low:high, :LANES]
            query = jnp.where(head_mask(query.shape, head), query, 0).astype(bf16)
            value = qkv_ref[:high, 2 * LANES :]
            value = jnp.where(head_mask(value.shape, head), value, 0).astype(bf16)
            scores = contract(query, qkv_ref[:high, LANES : 2 * LANES], 1, 1) * scale
            scores = jnp.where(row >= col, scores, -1e30)
            peak = jnp.max(scores, axis=1, keepdims=True)
            exponent = jnp.exp(scores - peak)
            inverse = 1.0 / jnp.sum(exponent, axis=1, keepdims=True)
            weights = (exponent * inverse).astype(bf16)
            total = total + jnp.dot(weights, value, preferred_element_type=f32)
        out_ref[low:high, :] = total.astype(bf16)


def attend(qkv):
    rows, columns = qkv.shape
    pairs = columns // (3 * LANES)
    return pl.pallas_call(
        attend_kernel,
        grid=(pairs,),
        in_specs=[pl.BlockSpec((rows, 3 * LANES), lambda p: (0, p))],
        out_specs=pl.BlockSpec((rows, LANES), lambda p: (0, p)),
        out_shape=jax.ShapeDtypeStruct((rows, pairs * LANES), bf16),
        compiler_params=pltpu.CompilerParams(vmem_limit_bytes=VMEM_BYTES),
        cost_estimate=pl.CostEstimate(
            flops=8 * rows * rows * pairs * LANES,
            bytes_accessed=8 * rows * pairs * LANES,
            transcendentals=2 * rows * rows * pairs,
        ),
        name="attend",
    )(qkv)


def attend_back_kernel(qkv_ref, grad_ref, cos_ref, sin_ref, out_ref, key_acc, value_acc):
    length = qkv_ref.shape[0]
    scale = HD ** (-0.5)
    key_acc[...] = jnp.zeros_like(key_acc)
    value_acc[...] = jnp.zeros_like(value_acc)
    for block in range(length // Q_ROWS):
        low, high = block * Q_ROWS, (block + 1) * Q_ROWS
        query_total = jnp.zeros((Q_ROWS, LANES), f32)
        key_row = lax.broadcasted_iota(jnp.int32, (high, Q_ROWS), 0)
        query_col = low + lax.broadcasted_iota(jnp.int32, (high, Q_ROWS), 1)
        for head in range(LANES // HD):
            query = qkv_ref[low:high, :LANES]
            query = jnp.where(head_mask(query.shape, head), query, 0).astype(bf16)
            grad = grad_ref[low:high, :]
            grad = jnp.where(head_mask(grad.shape, head), grad, 0).astype(bf16)
            keys = qkv_ref[:high, LANES : 2 * LANES]
            keys_own = jnp.where(head_mask(keys.shape, head), keys, 0).astype(bf16)
            scores = contract(keys, query, 1, 1) * scale
            scores = jnp.where(query_col >= key_row, scores, -1e30)
            peak = jnp.max(scores, axis=0, keepdims=True)
            exponent = jnp.exp(scores - peak)
            inverse = 1.0 / jnp.sum(exponent, axis=0, keepdims=True)
            weights = exponent * inverse
            grad_weights = contract(qkv_ref[:high, 2 * LANES :], grad, 1, 1)
            row_dot = jnp.sum(weights * grad_weights, axis=0, keepdims=True)
            grad_scores = (weights * (grad_weights - row_dot)).astype(bf16)
            value_acc[:high, :] += jnp.dot(weights.astype(bf16), grad, preferred_element_type=f32)
            key_acc[:high, :] += jnp.dot(grad_scores, query, preferred_element_type=f32)
            query_total = query_total + contract(grad_scores, keys_own, 0, 0)
        cosine, sine = cos_ref[low:high, :], sin_ref[low:high, :]
        out_ref[low:high, :LANES] = turn(query_total * scale, cosine, -sine).astype(bf16)
    out_ref[:, LANES : 2 * LANES] = turn(
        key_acc[...] * scale, cos_ref[...], -sin_ref[...]
    ).astype(bf16)
    out_ref[:, 2 * LANES :] = value_acc[...].astype(bf16)


def attend_back(qkv, grad_attended, cosine, sine):
    rows, columns = qkv.shape
    pairs = columns // (3 * LANES)
    return pl.pallas_call(
        attend_back_kernel,
        grid=(pairs,),
        in_specs=[
            pl.BlockSpec((rows, 3 * LANES), lambda p: (0, p)),
            pl.BlockSpec((rows, LANES), lambda p: (0, p)),
            pl.BlockSpec((rows, LANES), lambda p: (0, 0)),
            pl.BlockSpec((rows, LANES), lambda p: (0, 0)),
        ],
        out_specs=pl.BlockSpec((rows, 3 * LANES), lambda p: (0, p)),
        out_shape=jax.ShapeDtypeStruct((rows, columns), bf16),
        scratch_shapes=[pltpu.VMEM((rows, LANES), f32), pltpu.VMEM((rows, LANES), f32)],
        compiler_params=pltpu.CompilerParams(vmem_limit_bytes=VMEM_BYTES),
        cost_estimate=pl.CostEstimate(
            flops=20 * rows * rows * pairs * LANES,
            bytes_accessed=14 * rows * pairs * LANES,
            transcendentals=2 * rows * rows * pairs,
        ),
        name="attend_back",
    )(qkv, grad_attended, cosine, sine)


def feed_kernel(n_ref, c_ref, w_ref, *rest):
    outs = rest[-8:]
    n_out, c_out, inner_out, grad_out, ffn_out, back_out, ffn_acc, back_acc = outs
    step = pl.program_id(0)
    width = inner_out.shape[1]
    piece = n_out.shape[1]
    normed, cot = n_ref[...], c_ref[...]
    both = jnp.dot(normed, w_ref[:, : 2 * width], preferred_element_type=f32)
    gate, up = both[:, :width], both[:, width:]
    d_inner = jnp.dot(cot, w_ref[:, 2 * width :], preferred_element_type=f32)
    sigmoid = jax.nn.sigmoid(gate)
    silu = gate * sigmoid
    inner = (silu * up).astype(bf16)
    d_gate = (d_inner * up * sigmoid * (1.0 + gate * (1.0 - sigmoid))).astype(bf16)
    d_up = (d_inner * silu).astype(bf16)
    inner_out[...] = inner
    grad_out[:, :width] = d_gate
    grad_out[:, width:] = d_up
    start = pl.multiple_of(step * piece, piece)
    n_out[...] = n_ref[:, pl.ds(start, piece)]
    c_out[...] = c_ref[:, pl.ds(start, piece)]
    ffn = contract(inner, w_ref[:, 2 * width :], 1, 1)
    back = contract(grad_out[...], w_ref[:, : 2 * width], 1, 1)

    @pl.when(step == 0)
    def _():
        ffn_acc[...] = ffn
        back_acc[...] = back

    @pl.when(step > 0)
    def _():
        ffn_acc[...] += ffn
        back_acc[...] += back

    @pl.when(step == pl.num_programs(0) - 1)
    def _():
        ffn_out[...] = ffn_acc[...].astype(bf16)
        back_out[...] = back_acc[...].astype(bf16)


def feed(normed, cot, weights, slot, slots, kept):
    rows, width = normed.shape
    hidden = weights.shape[1] // 3
    steps = hidden // HID_TILE
    piece = width // steps
    in_specs = [
        pl.BlockSpec((rows, width), lambda n: (0, 0)),
        pl.BlockSpec((rows, width), lambda n: (0, 0)),
        pl.BlockSpec((width, 3 * HID_TILE), lambda n: (0, n)),
    ]
    args = [normed, cot, weights]
    aliases = {}
    if kept is not None:
        for index, array in enumerate(kept):
            aliases[len(args)] = index
            args.append(array)
            in_specs.append(pl.BlockSpec(memory_space=pl.ANY))
    total = rows * slots
    outs = pl.pallas_call(
        feed_kernel,
        grid=(steps,),
        in_specs=in_specs,
        out_specs=[
            pl.BlockSpec((rows, piece), lambda n: (slot, n)),
            pl.BlockSpec((rows, piece), lambda n: (slot, n)),
            pl.BlockSpec((rows, HID_TILE), lambda n: (slot, n)),
            pl.BlockSpec((rows, 2 * HID_TILE), lambda n: (slot, n)),
            pl.BlockSpec((rows, width), lambda n: (0, 0)),
            pl.BlockSpec((rows, width), lambda n: (0, 0)),
        ],
        out_shape=[
            jax.ShapeDtypeStruct((total, width), bf16),
            jax.ShapeDtypeStruct((total, width), bf16),
            jax.ShapeDtypeStruct((total, hidden), bf16),
            jax.ShapeDtypeStruct((total, 2 * hidden), bf16),
            jax.ShapeDtypeStruct((rows, width), bf16),
            jax.ShapeDtypeStruct((rows, width), bf16),
        ],
        scratch_shapes=[pltpu.VMEM((rows, width), f32), pltpu.VMEM((rows, width), f32)],
        input_output_aliases=aliases,
        compiler_params=pltpu.CompilerParams(vmem_limit_bytes=VMEM_BYTES),
        cost_estimate=pl.CostEstimate(
            flops=12 * rows * width * hidden,
            bytes_accessed=2 * (3 * width * hidden + 8 * rows * width + 3 * rows * hidden),
            transcendentals=rows * hidden,
        ),
        name="feed",
    )(*args)
    return tuple(outs[:4]), outs[4], outs[5]


def interleave(arrays, tile):
    pieces = []
    for start in range(0, arrays[0].shape[1], tile):
        pieces += [array[:, start : start + tile] for array in arrays]
    return jnp.concatenate(pieces, axis=1)


def take_apart(array, tile, count):
    pieces = [array[:, start : start + tile] for start in range(0, array.shape[1], tile)]
    return [jnp.concatenate(pieces[index::count], axis=1) for index in range(count)]


def make_layer(n_dp, n_t):
    def halve(vector):
        for axis, size in (("dp", n_dp), ("tensor", n_t)):
            index = lax.axis_index(axis)
            bit = size // 2
            while bit:
                parts = vector.reshape(2, -1)
                own = (index // bit) % 2
                keep = lax.dynamic_index_in_dim(parts, own, 0, keepdims=False)
                send = lax.dynamic_index_in_dim(parts, 1 - own, 0, keepdims=False)
                vector = keep + lax.ppermute(send, axis, [(i, i ^ bit) for i in range(size)])
                bit //= 2
        return vector

    def on_device(
        inputs, w_query, w_key, w_value, w_out, gain_one, w_gate, w_up, w_down, gain_two, cotangent
    ):
        rows = inputs.shape[0]
        group = LEN // rows
        sequences = n_t // group
        block_cols = w_query.shape[1]
        t = lax.axis_index("tensor")
        g = t % group
        group_ring = [(i, i - i % group + (i % group + 1) % group) for i in range(n_t)]
        ring = [(i, (i + 1) % n_t) for i in range(n_t)]

        def shift(array, amount):
            return lax.ppermute(array, "tensor", [(i, (i + amount) % n_t) for i in range(n_t)])

        def gather_group(own):
            whole = jnp.zeros((group * rows, own.shape[1]), own.dtype)
            block = own
            for step in range(group):
                if step:
                    block = lax.ppermute(block, "tensor", group_ring)
                place = ((g - step) % group) * rows
                whole = lax.dynamic_update_slice(whole, block, (place, 0))
            return whole

        def scatter_group(partial):
            carried = None
            for step in range(group - 1):
                part = partial((g - 1 - step) % group)
                if carried is not None:
                    part = part + carried.astype(f32)
                carried = lax.ppermute(part.astype(bf16), "tensor", group_ring)
            own = partial(g)
            return own if carried is None else own + carried.astype(f32)

        qkv_shard = interleave([w_query, w_key, w_value], LANES)
        att_shard = jnp.concatenate([qkv_shard, w_out.T], axis=1)
        att_full = [
            lax.all_gather(
                att_shard if not j else shift(att_shard, -group * j), "dp", axis=0, tiled=True
            )
            for j in range(sequences)
        ]
        feed_full = lax.all_gather(
            interleave([w_gate, w_up, w_down.T], HID_TILE), "dp", axis=0, tiled=True
        )
        gains = lax.all_gather(jnp.stack([gain_one, gain_two]), "dp", axis=1, tiled=True)
        gain_one_f, gain_two_f = gains[0].astype(f32), gains[1].astype(f32)

        features = inputs.astype(f32)
        normed_one = gather_group(rms_scale(features, gain_one_f).astype(bf16))
        cosine, sine = rope_tables()
        qkv = [project(normed_one, full, 3 * block_cols, cosine, sine) for full in att_full]
        attended = [attend(block) for block in qkv]
        out_t = [full[:, 3 * block_cols :] for full in att_full]
        qkv_w = [full[:, : 3 * block_cols] for full in att_full]

        def mix(block):
            total = None
            for att, weight in zip(attended, out_t):
                part = contract(lax.dynamic_slice_in_dim(att, block * rows, rows, 0), weight, 1, 1)
                total = part if total is None else total + part
            return total

        hidden_state = features + scatter_group(mix)

        normed = rms_scale(hidden_state, gain_two_f).astype(bf16)
        cot = cotangent
        kept = None
        ffn_parts, back_parts = [], []
        for step in range(n_t):
            if step:
                normed = lax.ppermute(normed, "tensor", ring)
                cot = lax.ppermute(cot, "tensor", ring)
            kept, ffn, back = feed(normed, cot, feed_full, step, n_t, kept)
            ffn_parts.append(ffn)
            back_parts.append(back)

        def scatter_ring(parts):
            carried = None
            for part in parts[1:]:
                part = part.astype(f32)
                if carried is not None:
                    part = part + carried.astype(f32)
                carried = lax.ppermute(part.astype(bf16), "tensor", ring)
            own = parts[0].astype(f32)
            return own if carried is None else own + carried.astype(f32)

        d_normed_two = scatter_ring(back_parts)
        output = (hidden_state + scatter_ring(ffn_parts)).astype(bf16)
        n_all, c_all, inner_all, grad_all = kept
        grad_gate_up = lax.psum_scatter(
            contract(n_all, grad_all, 0, 0).astype(bf16), "dp", scatter_dimension=0, tiled=True
        )
        grad_down_t = lax.psum_scatter(
            contract(c_all, inner_all, 0, 0).astype(bf16), "dp", scatter_dimension=0, tiled=True
        )

        hidden_grad, gain_two_part = norm_back(hidden_state, gain_two_f, d_normed_two)
        d_hidden = cotangent.astype(f32) + hidden_grad

        d_mixed = gather_group(d_hidden.astype(bf16))
        d_qkv, grad_qkv = [None] * sequences, [None] * sequences
        grad_out_t = lax.psum_scatter(
            jnp.concatenate([contract(d_mixed, att, 0, 0).astype(bf16) for att in attended], axis=1),
            "dp",
            scatter_dimension=0,
            tiled=True,
        )
        for j in reversed(range(sequences)):
            d_attended = jnp.dot(d_mixed, out_t[j], preferred_element_type=f32).astype(bf16)
            d_qkv[j] = attend_back(qkv[j], d_attended, cosine, sine)
            grad_qkv[j] = lax.psum_scatter(
                contract(normed_one, d_qkv[j], 0, 0).astype(bf16),
                "dp",
                scatter_dimension=0,
                tiled=True,
            )

        def mix_back(block):
            total = None
            for grad, weight in zip(d_qkv, qkv_w):
                part = contract(lax.dynamic_slice_in_dim(grad, block * rows, rows, 0), weight, 1, 1)
                total = part if total is None else total + part
            return total

        d_normed_one = scatter_group(mix_back)
        feature_grad, gain_one_part = norm_back(features, gain_one_f, d_normed_one)
        input_grad = d_hidden + feature_grad

        qkv_sum = grad_qkv[0].astype(f32)
        out_sum = grad_out_t[:, :block_cols].astype(f32)
        for j in range(1, sequences):
            qkv_sum = qkv_sum + shift(grad_qkv[j], group * j).astype(f32)
            piece = grad_out_t[:, j * block_cols : (j + 1) * block_cols]
            out_sum = out_sum + shift(piece, group * j).astype(f32)
        grad_query, grad_key, grad_value = take_apart(qkv_sum, LANES, 3)
        grad_gate, grad_up = take_apart(grad_gate_up.astype(f32), HID_TILE, 2)
        return (
            output,
            input_grad,
            grad_query,
            grad_key,
            grad_value,
            out_sum.T,
            halve(gain_one_part),
            grad_gate,
            grad_up,
            grad_down_t.astype(f32).T,
            halve(gain_two_part),
        )

    return on_device


def solution(mesh):
    return jax.shard_map(
        make_layer(mesh.shape["dp"], mesh.shape["tensor"]),
        mesh=mesh,
        in_specs=(
            P(("dp", "tensor"), None),
            P("dp", "tensor"),
            P("dp", "tensor"),
            P("dp", "tensor"),
            P("tensor", "dp"),
            P("dp"),
            P("dp", "tensor"),
            P("dp", "tensor"),
            P("tensor", "dp"),
            P("dp"),
            P(("dp", "tensor"), None),
        ),
        out_specs=(
            P(("dp", "tensor"), None),
            P(("dp", "tensor"), None),
            P("dp", "tensor"),
            P("dp", "tensor"),
            P("dp", "tensor"),
            P("tensor", "dp"),
            P(("dp", "tensor")),
            P("dp", "tensor"),
            P("dp", "tensor"),
            P("tensor", "dp"),
            P(("dp", "tensor")),
        ),
        check_vma=False,
    )
```

time: 2270 us -> 1200 us (0.53)
  waiting for transfers between devices: 1310 us -> 596 us
  matrix products: 508 us -> 152 us
  Pallas kernels: 0 us -> 284 us
  local copies, waits for them, and re-layouts: 207 us -> 63.6 us
  other arithmetic: 126 us -> 49.5 us
  blocking collectives: 65.5 us -> 8.99 us
    all_gather x12 -> x3, waiting for transfers between devices: 698 us -> 0.01 us  [the longest x2 0.01 us: on_device(): lax.all_gather(att_shard if not j else shift(att_shard, -group * j), 'dp'...]
    ppermute x0 -> x29, waiting for transfers between devices: none -> 596 us  [the longest x6 138 us: scatter_ring(): carried = lax.ppermute(part.astype(bf16), 'tensor', ring)]
    reduce_scatter x10 -> x5, waiting for transfers between devices: 522 us -> 0.02 us  [the longest x2 0.01 us: on_device(): lax.psum_scatter(contract(normed_one, d_qkv[j], 0, 0).astype(bf16), 'dp',...]
    pallas_call x0 -> x10, Pallas kernels: none -> 284 us  [the longest x4 165 us: feed(): pl.pallas_call(feed_kernel, grid=(steps,), in_specs=in_specs, out_specs=[...]
    dot_general x35 -> x2, matrix products: 266 us -> 11.2 us  [on_device(): jnp.dot(d_mixed, out_t[j], preferred_element_type=f32).astype(bf16)]
    dot_general x14, matrix products: 242 us -> 140 us  [contract(): lax.dot_general(left, right, (((left_dim,), (right_dim,)), ((), ())), pre...]
    dynamic_update_slice x8 -> x2, local copies, waits for them, and re-layouts: 91.1 us -> 3.42 us  [gather_group(): whole = lax.dynamic_update_slice(whole, block, (place, 0))]
    all_to_all x1 -> x0, waiting for transfers between devices: 80 us -> none  [on_device(): lax.all_to_all(attended, 'tensor', split_axis=0, concat_axis=1, tiled=True)]
  transfers between devices with their start and end apart: 23 -> 37, of which waited for: 15 -> 20; matrix products, arithmetic and copies ran while one was open for 32% -> 18% of each run, Pallas kernels for 0% -> 21%
where the time goes in v1:
time: 1200 us
  waiting for transfers between devices  596 us (50%)
  Pallas kernels  284 us (24%)
  matrix products  152 us (13%)
  local copies, waits for them, and re-layouts  63.6 us (5%)
  other arithmetic  49.5 us (4%)
  starting transfers between devices  29.1 us (2%)
  between operations  15.2 us (1%)
    pallas_call x4, Pallas kernels, feed(): pl.pallas_call(feed_kernel, grid=(steps,), in_specs=in_specs, out_specs=[...  165 us
    dot_general x14, matrix products, contract(): lax.dot_general(left, right, (((left_dim,), (right_dim,)), ((), ())), pre...  140 us
    ppermute x6, waiting for transfers between devices, scatter_ring(): carried = lax.ppermute(part.astype(bf16), 'tensor', ring)  138 us
    ppermute x3, waiting for transfers between devices, on_device(): normed = lax.ppermute(normed, 'tensor', ring)  89.8 us
    ppermute x2, waiting for transfers between devices, gather_group(): block = lax.ppermute(block, 'tensor', group_ring)  88.4 us
    ppermute x3, waiting for transfers between devices, shift(): lax.ppermute(array, 'tensor', [(i, (i + amount) % n_t) for i in range(n_t)])  84 us
    ppermute x3, waiting for transfers between devices, on_device(): cot = lax.ppermute(cot, 'tensor', ring)  83.2 us
    ppermute x2, waiting for transfers between devices, scatter_group(): carried = lax.ppermute(part.astype(bf16), 'tensor', group_ring)  77.2 us
  transfers between devices with their start and end apart: 37, of which 20 were waited for; matrix products, arithmetic and copies ran while one was open for 18% of the time, Pallas kernels for 21%

profile of v1, /device:TPU:0, one launch (start us, length us, event | category | flops | bytes accessed | tf_op | source)
XLA Modules:
  0.0 1197.9 jit_solution(2048608726349906566)
XLA Ops:
  19.9 4.1 collective-permute-start.1
  24.0 45.8 %collective-permute-done.1 = bf16[256,2048]{1,0:T(8,128)(2,1)S(1)} collective-permute-done((bf16[256,2048]{1,0:T(8,128)(2,1)}, bf16[256,2048]{1,0:T(8,128)(2,1)S(1)}, u32[]{:S(2)}, u32[]{:S(2)}) %collective-permute-start.1) | collective-permute-done | bytes 1048608 | tf_op jit(solution)/shard_map/ppermute | solution.py:333
  100.2 9.0 all_gather.12
  110.3 2.5 broadcast.77.clone
  112.9 2.5 constant_dynamic-update-slice_fusion.15
  116.3 1.9 fusion.45
  120.0 43.6 %collective-permute-done = bf16[512,2048]{1,0:T(8,128)(2,1)} collective-permute-done((bf16[512,2048]{1,0:T(8,128)(2,1)}, bf16[512,2048]{1,0:T(8,128)(2,1)}, u32[]{:S(2)}, u32[]{:S(2)}) %collective-permute-start) | collective-permute-done | bytes 2097184 | tf_op jit(solution)/shard_map/ppermute | solution.py:340
  163.6 3.2 constant_dynamic-update-slice_fusion.14.x_ref
  166.8 16.2 %project.2.qkv_ref = bf16[1024,1536]{1,0:T(8,128)(2,1)} custom-call(bf16[1024,2048]{1,0:T(8,128)(2,1)} %constant_dynamic-update-slice_fusion.14.x_ref, bf16[2048,2048]{1,0:T(8,128)(2,1)} %all-gather.4.cloned.1.call-done.w_ref, f32[1024,128]{1,0:T(8,128)} %get-tuple-element.139.cos_ref, f32[1024,128]{1,0:T(8,128)} %get-tuple-element.140.sin_ref), custom_call_target="tpu_custom_call" | custom-call | flops 6442450944 | bytes 13631488 | tf_op jit(solution)/shard_map/project/pallas_call | solution.py:73
  183.0 14.9 %attend.2 = bf16[1024,512]{1,0:T(8,128)(2,1)} custom-call(bf16[1024,1536]{1,0:T(8,128)(2,1)} %project.2.qkv_ref), custom_call_target="tpu_custom_call" | custom-call | flops 4294967296 | bytes 4194304 | tf_op jit(solution)/shard_map/attend/pallas_call | solution.py:125
  198.0 15.8 %project.3.qkv_ref = bf16[1024,1536]{1,0:T(8,128)(2,1)} custom-call(bf16[1024,2048]{1,0:T(8,128)(2,1)} %constant_dynamic-update-slice_fusion.14.x_ref, bf16[2048,2048]{1,0:T(8,128)(2,1)} %all-gather.6.cloned.1.call-done.w_ref, f32[1024,128]{1,0:T(8,128)} %get-tuple-element.139.cos_ref, f32[1024,128]{1,0:T(8,128)} %get-tuple-element.140.sin_ref), custom_call_target="tpu_custom_call" | custom-call | flops 6442450944 | bytes 13631488 | tf_op jit(solution)/shard_map/project/pallas_call | solution.py:73
  213.7 14.9 %attend.3 = bf16[1024,512]{1,0:T(8,128)(2,1)} custom-call(bf16[1024,1536]{1,0:T(8,128)(2,1)} %project.3.qkv_ref), custom_call_target="tpu_custom_call" | custom-call | flops 4294967296 | bytes 4194304 | tf_op jit(solution)/shard_map/attend/pallas_call | solution.py:125
  228.6 3.1 fusion.23
  231.8 4.2 add_convert_fusion.6
  238.1 3.0 fusion.25
  241.2 42.3 %collective-permute-done.2 = bf16[512,2048]{1,0:T(8,128)(2,1)} collective-permute-done((bf16[512,2048]{1,0:T(8,128)(2,1)}, bf16[512,2048]{1,0:T(8,128)(2,1)}, u32[]{:S(2)}, u32[]{:S(2)}) %collective-permute-start.2) | collective-permute-done | bytes 2097184 | tf_op jit(solution)/shard_map/ppermute | solution.py:351
  283.5 4.0 multiply_reduce_fusion.2
  289.5 2.5 collective-permute-start.3
  292.0 39.5 %collective-permute-done.6.c_ref = bf16[512,2048]{1,0:T(8,128)(2,1)} collective-permute-done((bf16[512,2048]{1,0:T(8,128)(2,1)}, bf16[512,2048]{1,0:T(8,128)(2,1)}, u32[]{:S(2)}, u32[]{:S(2)}) %collective-permute-start.6) | collective-permute-done | bytes 2097184 | tf_op jit(solution)/shard_map/ppermute | solution.py:393
  331.5 44.8 %collective-permute-done.3.n_ref = bf16[512,2048]{1,0:T(8,128)(2,1)S(1)} collective-permute-done((bf16[512,2048]{1,0:T(8,128)(2,1)S(1)}, bf16[512,2048]{1,0:T(8,128)(2,1)S(1)}, u32[]{:S(2)}, u32[]{:S(2)}) %collective-permute-start.3) | collective-permute-done | bytes 2097184 | tf_op jit(solution)/shard_map/ppermute | solution.py:392
  377.7 43.7 %collective-permute-done.7.c_ref = bf16[512,2048]{1,0:T(8,128)(2,1)} collective-permute-done((bf16[512,2048]{1,0:T(8,128)(2,1)}, bf16[512,2048]{1,0:T(8,128)(2,1)}, u32[]{:S(2)}, u32[]{:S(2)}) %collective-permute-start.7) | collective-permute-done | bytes 2097184 | tf_op jit(solution)/shard_map/ppermute | solution.py:393
  421.4 44.9 %collective-permute-done.4.n_ref = bf16[512,2048]{1,0:T(8,128)(2,1)} collective-permute-done((bf16[512,2048]{1,0:T(8,128)(2,1)S(1)}, bf16[512,2048]{1,0:T(8,128)(2,1)}, u32[]{:S(2)}, u32[]{:S(2)}) %collective-permute-start.4) | collective-permute-done | bytes 2097184 | tf_op jit(solution)/shard_map/ppermute | solution.py:392
  466.3 41.3 %feed.4 = (bf16[2048,2048]{1,0:T(8,128)(2,1)}, bf16[2048,2048]{1,0:T(8,128)(2,1)}, bf16[2048,2048]{1,0:T(8,128)(2,1)}, bf16[2048,4096]{1,0:T(8,128)(2,1)}, bf16[...) custom-call(bf16[512,2048]{1,0:T(8,128)(2,1)} %copy-done.10, bf16[512,2048]{1,0:T(8,128)(2,1)} %c_ref.1, ...), custom_call_target="tpu_custom_call" | custom-call | flops 25769803776 | bytes 48234496 | tf_op jit(solution)/shard_map/feed/pallas_call | solution.py:261
  507.6 41.3 %feed.5 = (bf16[2048,2048]{1,0:T(8,128)(2,1)}, bf16[2048,2048]{1,0:T(8,128)(2,1)}, bf16[2048,2048]{1,0:T(8,128)(2,1)}, bf16[2048,4096]{1,0:T(8,128)(2,1)}, bf16[...) custom-call(bf16[512,2048]{1,0:T(8,128)(2,1)} %copy-done.32, ...), custom_call_target="tpu_custom_call", output_to_operand_aliasing={{0}: (3, {}), {1}: (4, {}), {2}: (5, {}), {3}: (6, {})} | custom-call | flops 25769803776 | bytes 48234496 | tf_op jit(solution)/shard_map/feed/pallas_call | solution.py:261
  549.4 41.2 %feed.6 = (bf16[2048,2048]{1,0:T(8,128)(2,1)}, bf16[2048,2048]{1,0:T(8,128)(2,1)}, bf16[2048,2048]{1,0:T(8,128)(2,1)}, bf16[2048,4096]{1,0:T(8,128)(2,1)}, bf16[...) custom-call(bf16[512,2048]{1,0:T(8,128)(2,1)} %collective-permute-do, ...), custom_call_target="tpu_custom_call", output_to_operand_aliasing={{0}: (3, {}), {1}: (4, {}), {2}: (5, {}), {3}: (6, {})} | custom-call | flops 25769803776 | bytes 48234496 | tf_op jit(solution)/shard_map/feed/pallas_call | solution.py:261
  590.6 9.3 collective-permute-done.12
  601.2 3.1 add_convert_fusion.2
  604.4 41.2 %feed.7 = (bf16[2048,2048]{1,0:T(8,128)(2,1)}, bf16[2048,2048]{1,0:T(8,128)(2,1)}, bf16[2048,2048]{1,0:T(8,128)(2,1)}, bf16[2048,4096]{1,0:T(8,128)(2,1)}, bf16[...) custom-call(bf16[512,2048]{1,0:T(8,128)(2,1)} %collective-permute-do, ...), custom_call_target="tpu_custom_call", output_to_operand_aliasing={{0}: (3, {}), {1}: (4, {}), {2}: (5, {}), {3}: (6, {})} | custom-call | flops 25769803776 | bytes 48234496 | tf_op jit(solution)/shard_map/feed/pallas_call | solution.py:261
  645.7 7.1 collective-permute-done.13
  652.8 3.2 add_convert_fusion.1
  656.5 47.4 %collective-permute-done.14 = bf16[512,2048]{1,0:T(8,128)(2,1)S(1)} collective-permute-done((bf16[512,2048]{1,0:T(8,128)(2,1)S(1)}, bf16[512,2048]{1,0:T(8,128)(2,1)S(1)}, u32[]{:S(2)}, u32[]{:S(2)}) %collective-permute-start.14) | collective-permute-done | bytes 2097184 | tf_op jit(solution)/shard_map/ppermute | solution.py:404
  706.0 3.5 constant_dynamic-update-slice_fusion.13
  709.6 44.8 %collective-permute-done.15 = bf16[512,2048]{1,0:T(8,128)(2,1)S(1)} collective-permute-done((bf16[512,2048]{1,0:T(8,128)(2,1)S(1)}, bf16[512,2048]{1,0:T(8,128)(2,1)S(1)}, u32[]{:S(2)}, u32[]{:S(2)}) %collective-permute-start.15) | collective-permute-done | bytes 2097184 | tf_op jit(solution)/shard_map/ppermute | solution.py:340
  754.7 1.9 copy-done.6
  756.6 5.0 fusion.38.grad_ref
  761.6 28.3 %attend_back.3 = bf16[1024,1536]{1,0:T(8,128)(2,1)} custom-call(bf16[1024,1536]{1,0:T(8,128)(2,1)} %project.3.qkv_ref, bf16[1024,512]{1,0:T(8,128)(2,1)} %fusion.38.grad_ref, f32[1024,128]{1,0:T(8,128)} %get-tuple-element.139.cos_ref, f32[1024,128]{1,0:T(8,128)} %get-tuple-element.140.sin_ref), custom_call_target="tpu_custom_call" | custom-call | flops 10737418240 | bytes 7340032 | tf_op jit(solution)/shard_map/attend_back/pallas_call | solution.py:181
  789.9 11.7 convolution_convert_fusion.2
  802.9 5.2 convolution_convert_fusion.5
  808.1 2.5 convolution_convert_fusion.4
  810.6 2.6 pad_maximum_fusion
  813.3 23.9 %convolution_convert_fusion.1 = bf16[2048,2048]{1,0:T(8,128)(2,1)} fusion(bf16[2048,2048]{1,0:T(8,128)(2,1)} %get-tuple-element.57, bf16[2048,2048]{1,0:T(8,128)(2,1)} %get-tuple-element.58), kind=kOutput, calls=%fused_computation.6 | convolution fusion | flops 17184063488 | bytes 25165824 | tf_op jit(solution)/shard_map/dot_general | solution.py:33
  837.3 6.2 fusion.35.grad_ref
  843.6 28.5 %attend_back.2 = bf16[1024,1536]{1,0:T(8,128)(2,1)} custom-call(bf16[1024,1536]{1,0:T(8,128)(2,1)} %project.2.qkv_ref, bf16[1024,512]{1,0:T(8,128)(2,1)} %fusion.35.grad_ref, f32[1024,128]{1,0:T(8,128)} %get-tuple-element.139.cos_ref, f32[1024,128]{1,0:T(8,128)} %get-tuple-element.140.sin_ref), custom_call_target="tpu_custom_call" | custom-call | flops 10737418240 | bytes 7340032 | tf_op jit(solution)/shard_map/attend_back/pallas_call | solution.py:181
  872.1 12.1 %convolution_convert_fusion.3 = bf16[2048,1536]{1,0:T(8,128)(2,1)} fusion(bf16[1024,2048]{1,0:T(8,128)(2,1)} %constant_dynamic-update-slice_fusion.14.x_ref, bf16[1024,1536]{1,0:T(8,128)(2,1)} %attend_back.2), kind=kOutput, calls=%fused_computation.8 | convolution fusion | flops 6445596672 | bytes 13631488 | tf_op jit(solution)/shard_map/dot_general | solution.py:33
  884.2 43.1 %convolution_convert_fusion = bf16[2048,4096]{1,0:T(8,128)(2,1)} fusion(bf16[2048,2048]{1,0:T(8,128)(2,1)} %get-tuple-element.55, bf16[2048,4096]{1,0:T(8,128)(2,1)} %get-tuple-element.56), kind=kOutput, calls=%fused_computation | convolution fusion | flops 34368126976 | bytes 41943040 | tf_op jit(solution)/shard_map/dot_general | solution.py:33
  927.9 45.4 %collective-permute-done.9 = bf16[512,2048]{1,0:T(8,128)(2,1)} collective-permute-done((bf16[512,2048]{1,0:T(8,128)(2,1)}, bf16[512,2048]{1,0:T(8,128)(2,1)}, u32[]{:S(2)}, u32[]{:S(2)}) %collective-permute-start.9) | collective-permute-done | bytes 2097184 | tf_op jit(solution)/shard_map/ppermute | solution.py:404
  973.3 3.7 add_convert_fusion.5
  977.0 6.2 fusion
  983.2 7.8 add_convert_fusion
  992.7 2.0 collective-permute-done.24
  996.4 2.0 collective-permute-done.25
  998.5 29.1 %collective-permute-done.10 = bf16[512,2048]{1,0:T(8,128)(2,1)} collective-permute-done((bf16[512,2048]{1,0:T(8,128)(2,1)}, bf16[512,2048]{1,0:T(8,128)(2,1)}, u32[]{:S(2)}, u32[]{:S(2)}) %collective-permute-start.10) | collective-permute-done | bytes 2097184 | tf_op jit(solution)/shard_map/ppermute | solution.py:404
  1027.6 3.8 add_convert_fusion.4
  1031.7 5.9 fusion.2
  1037.7 34.9 %collective-permute-done.16 = bf16[512,2048]{1,0:T(8,128)(2,1)} collective-permute-done((bf16[512,2048]{1,0:T(8,128)(2,1)}, bf16[512,2048]{1,0:T(8,128)(2,1)}, u32[]{:S(2)}, u32[]{:S(2)}) %collective-permute-start.16) | collective-permute-done | bytes 2097184 | tf_op jit(solution)/shard_map/ppermute | solution.py:351
  1072.6 7.5 fusion.11
  1081.8 26.2 %collective-permute-done.27 = f32[128]{0:T(128)S(1)} collective-permute-done((f32[128]{0:T(128)S(1)}, f32[128]{0:T(128)S(1)}, u32[]{:S(2)}, u32[]{:S(2)}) %collective-permute-start.27) | collective-permute-done | bytes 544 | tf_op jit(solution)/shard_map/ppermute | solution.py:316
  1109.9 4.5 collective-permute-start.28
  1117.4 3.6 collective-permute-done.22
  1121.1 2.0 collective-permute-start.23
  1123.1 10.6 fusion.13
  1136.2 2.7 collective-permute-start.18
  1142.3 38.2 %collective-permute-done.18 = bf16[256,512]{0,1:T(8,128)(2,1)} collective-permute-done((bf16[256,512]{0,1:T(8,128)(2,1)}, bf16[256,512]{0,1:T(8,128)(2,1)}, u32[]{:S(2)}, u32[]{:S(2)}) %collective-permute-start.18) | collective-permute-done | bytes 262176 | tf_op jit(solution)/shard_map/ppermute | solution.py:333
  1186.3 2.1 convert_element_type.185
  (240 shorter events, 83.2 us)
Async XLA Ops:
  7.2 159.6 %all-gather.4.cloned.1.call-start = ((), (), s32[]{:S(2)}) async-start(), calls=%async_computation.5 | async-start | bytes 9437184 | tf_op jit(solution)/shard_map/all_gather | solution.py:358
  10.7 61.7 %copy-start.15 = (bf16[256,2048]{1,0:T(8,128)(2,1)S(1)}, bf16[256,2048]{1,0:T(8,128)(2,1)}, u32[]{:S(2)}) copy-start(bf16[256,2048]{1,0:T(8,128)(2,1)} %param.17) | copy-start | bytes 3145732
  19.8 178.1 %all-gather.6.cloned.1.call-start = ((), (), s32[]{:S(2)}) async-start(), calls=%async_computation.6 | async-start | bytes 9437184 | tf_op jit(solution)/shard_map/all_gather | solution.py:358
  19.9 50.0 %collective-permute-start.1 = (bf16[256,2048]{1,0:T(8,128)(2,1)}, bf16[256,2048]{1,0:T(8,128)(2,1)S(1)}, u32[]{:S(2)}, u32[]{:S(2)}) collective-permute-start(bf16[256,2048]{1,0:T(8,128)(2,1)} %copy-done.12), channel_id=1, source_target_pairs={{0,2},{1,3},{2,0},{3,1},{4,6},{5,7},{6,4},{7,5},{8,10},{9,11},{10,... | collective-permute-start | bytes 3145736 | tf_op jit(solution)/shard_map/ppermute | solution.py:333
  70.8 395.5 %all-gather.8.cloned.1.call-start = ((), (), s32[]{:S(2)}) async-start(), calls=%async_computation.7 | async-start | bytes 28311552 | tf_op jit(solution)/shard_map/all_gather | solution.py:363
  84.3 15.9 %copy-start.33 = (bf16[256]{0:T(256)(128)(2,1)S(1)}, bf16[256]{0:T(256)(128)(2,1)}, u32[]{:S(2)}) copy-start(bf16[256]{0:T(256)(128)(2,1)} %param.20) | copy-start | bytes 1540
  84.3 15.9 %copy-start.34 = (bf16[256]{0:T(256)(128)(2,1)S(1)}, bf16[256]{0:T(256)(128)(2,1)}, u32[]{:S(2)}) copy-start(bf16[256]{0:T(256)(128)(2,1)} %param.16) | copy-start | bytes 1540
  84.3 24.9 %copy-start.2 = (bf16[512,2048]{1,0:T(8,128)(2,1)S(1)}, bf16[512,2048]{1,0:T(8,128)(2,1)}, u32[]{:S(2)}) copy-start(bf16[512,2048]{1,0:T(8,128)(2,1)} %param.11) | copy-start | bytes 6291460
  100.1 1033.7 %reduce-scatter.8.cloned.1.call-start = ((), (), s32[]{:S(2)}) async-start(), calls=%async_computation.9 | async-start | bytes 7077888 | tf_op jit(solution)/shard_map/reduce_scatter | solution.py:432
  110.3 5.1 copy-start.28
  110.3 5.1 copy-start.20
  110.3 595.6 %copy-start.18 = (f32[1,2048]{1,0:T(1,128)}, f32[1,2048]{1,0:T(1,128)S(1)}, u32[]{:S(2)}) copy-start(f32[1,2048]{1,0:T(1,128)S(1)} %get-tuple-element.123) | copy-start | bytes 24580
  115.4 48.2 %collective-permute-start = (bf16[512,2048]{1,0:T(8,128)(2,1)}, bf16[512,2048]{1,0:T(8,128)(2,1)}, u32[]{:S(2)}, u32[]{:S(2)}) collective-permute-start(bf16[512,2048]{1,0:T(8,128)(2,1)} %get-tuple-element.88), channel_id=1, source_target_pairs={{0,1},{1,0},{2,3},{3,2},{4,5},{5,4},{6,7},{7,6},{8,9},{9,8},{10,11... | collective-permute-start | bytes 6291464 | tf_op jit(solution)/shard_map/ppermute | solution.py:340
  236.0 47.5 %collective-permute-start.2 = (bf16[512,2048]{1,0:T(8,128)(2,1)}, bf16[512,2048]{1,0:T(8,128)(2,1)}, u32[]{:S(2)}, u32[]{:S(2)}) collective-permute-start(bf16[512,2048]{1,0:T(8,128)(2,1)} %add_convert_fusion.6), channel_id=1, source_target_pairs={{0,1},{1,0},{2,3},{3,2},{4,5},{5,4},{6,7},{7,6},{8,9},{9,8},{10,11... | collective-permute-start | bytes 6291464 | tf_op jit(solution)/shard_map/ppermute | solution.py:351
  237.1 94.4 %collective-permute-start.6 = (bf16[512,2048]{1,0:T(8,128)(2,1)}, bf16[512,2048]{1,0:T(8,128)(2,1)}, u32[]{:S(2)}, u32[]{:S(2)}) collective-permute-start(bf16[512,2048]{1,0:T(8,128)(2,1)} %c_ref.1), channel_id=1, source_target_pairs={{0,1},{1,2},{2,3},{3,0},{4,5},{5,6},{6,7},{7,4},{8,9},{9,10},{10,1... | collective-permute-start | bytes 6291464 | tf_op jit(solution)/shard_map/ppermute | solution.py:393
  287.5 418.5 %copy-start.22 = (f32[512]{0:T(512)}, f32[512]{0:T(512)S(1)}, u32[]{:S(2)}) copy-start(f32[512]{0:T(512)S(1)} %fusion.55) | copy-start | bytes 6148
  289.5 176.8 %copy-start.10 = (bf16[512,2048]{1,0:T(8,128)(2,1)}, bf16[512,2048]{1,0:T(8,128)(2,1)S(1)}, u32[]{:S(2)}) copy-start(bf16[512,2048]{1,0:T(8,128)(2,1)S(1)} %multiply_convert_fusion.n_ref) | copy-start | bytes 6291460
  289.5 86.8 %collective-permute-start.3 = (bf16[512,2048]{1,0:T(8,128)(2,1)S(1)}, bf16[512,2048]{1,0:T(8,128)(2,1)S(1)}, u32[]{:S(2)}, u32[]{:S(2)}) collective-permute-start(bf16[512,2048]{1,0:T(8,128)(2,1)S(1)} %multiply_convert_fusion.n_ref), channel_id=1, source_target_pairs={{0,1},{1,2},{2,3},{3,0},{4,5},{5,6},{6,7},{7,4},{8,9},{9,10},{10,1... | collective-permute-start | bytes 6291464 | tf_op jit(solution)/shard_map/ppermute | solution.py:392
  331.5 89.9 %collective-permute-start.7 = (bf16[512,2048]{1,0:T(8,128)(2,1)}, bf16[512,2048]{1,0:T(8,128)(2,1)}, u32[]{:S(2)}, u32[]{:S(2)}) collective-permute-start(bf16[512,2048]{1,0:T(8,128)(2,1)} %collective-permute-done.6.c_ref), channel_id=1, source_target_pairs={{0,1},{1,2},{2,3},{3,0},{4,5},{5,6},{6,7},{7,4},{8,9},{9,10},{10,1... | collective-permute-start | bytes 6291464 | tf_op jit(solution)/shard_map/ppermute | solution.py:393
  377.7 88.7 %collective-permute-start.4 = (bf16[512,2048]{1,0:T(8,128)(2,1)S(1)}, bf16[512,2048]{1,0:T(8,128)(2,1)}, u32[]{:S(2)}, u32[]{:S(2)}) collective-permute-start(bf16[512,2048]{1,0:T(8,128)(2,1)S(1)} %collective-permute-done.3.n_ref), channel_id=1, source_target_pairs={{0,1},{1,2},{2,3},{3,0},{4,5},{5,6},{6,7},{7,4},{8,9},{9,10},{10,1... | collective-permute-start | bytes 6291464 | tf_op jit(solution)/shard_map/ppermute | solution.py:392
  421.4 183.0 %collective-permute-start.8 = (bf16[512,2048]{1,0:T(8,128)(2,1)}, bf16[512,2048]{1,0:T(8,128)(2,1)}, u32[]{:S(2)}, u32[]{:S(2)}) collective-permute-start(bf16[512,2048]{1,0:T(8,128)(2,1)} %collective-permute-done.7.c_ref), channel_id=1, source_target_pairs={{0,1},{1,2},{2,3},{3,0},{4,5},{5,6},{6,7},{7,4},{8,9},{9,10},{10,1... | collective-permute-start | bytes 6291464 | tf_op jit(solution)/shard_map/ppermute | solution.py:393
  466.3 138.1 %collective-permute-start.5 = (bf16[512,2048]{1,0:T(8,128)(2,1)}, bf16[512,2048]{1,0:T(8,128)(2,1)}, u32[]{:S(2)}, u32[]{:S(2)}) collective-permute-start(bf16[512,2048]{1,0:T(8,128)(2,1)} %collective-permute-done.4.n_ref), channel_id=1, source_target_pairs={{0,1},{1,2},{2,3},{3,0},{4,5},{5,6},{6,7},{7,4},{8,9},{9,10},{10,1... | collective-permute-start | bytes 6291464 | tf_op jit(solution)/shard_map/ppermute | solution.py:392
  548.9 51.0 %collective-permute-start.12 = (bf16[512,2048]{1,0:T(8,128)(2,1)}, bf16[512,2048]{1,0:T(8,128)(2,1)S(1)}, u32[]{:S(2)}, u32[]{:S(2)}) collective-permute-start(bf16[512,2048]{1,0:T(8,128)(2,1)} %get-tuple-element.54), channel_id=1, source_target_pairs={{0,1},{1,2},{2,3},{3,0},{4,5},{5,6},{6,7},{7,4},{8,9},{9,10},{10,1... | collective-permute-start | bytes 6291464 | tf_op jit(solution)/shard_map/ppermute | solution.py:404
  604.4 48.5 %collective-permute-start.13 = (bf16[512,2048]{1,0:T(8,128)(2,1)S(1)}, bf16[512,2048]{1,0:T(8,128)(2,1)}, u32[]{:S(2)}, u32[]{:S(2)}) collective-permute-start(bf16[512,2048]{1,0:T(8,128)(2,1)S(1)} %add_convert_fusion.2), channel_id=1, source_target_pairs={{0,1},{1,2},{2,3},{3,0},{4,5},{5,6},{6,7},{7,4},{8,9},{9,10},{10,1... | collective-permute-start | bytes 6291464 | tf_op jit(solution)/shard_map/ppermute | solution.py:404
  652.8 51.2 %copy-start.1 = (f32[512,2048]{1,0:T(8,128)S(1)}, f32[512,2048]{1,0:T(8,128)}, u32[]{:S(2)}) copy-start(f32[512,2048]{1,0:T(8,128)} %copy-done) | copy-start | bytes 12582916
  652.8 51.2 %copy-start.4 = (bf16[512,2048]{1,0:T(8,128)(2,1)S(1)}, bf16[512,2048]{1,0:T(8,128)(2,1)}, u32[]{:S(2)}) copy-start(bf16[512,2048]{1,0:T(8,128)(2,1)} %get-tuple-element.51) | copy-start | bytes 6291460
  656.0 48.0 %collective-permute-start.14 = (bf16[512,2048]{1,0:T(8,128)(2,1)S(1)}, bf16[512,2048]{1,0:T(8,128)(2,1)S(1)}, u32[]{:S(2)}, u32[]{:S(2)}) collective-permute-start(bf16[512,2048]{1,0:T(8,128)(2,1)S(1)} %add_convert_fusion.1), channel_id=1, source_target_pairs={{0,1},{1,2},{2,3},{3,0},{4,5},{5,6},{6,7},{7,4},{8,9},{9,10},{10,1... | collective-permute-start | bytes 6291464 | tf_op jit(solution)/shard_map/ppermute | solution.py:404
  709.5 44.9 %collective-permute-start.15 = (bf16[512,2048]{1,0:T(8,128)(2,1)S(1)}, bf16[512,2048]{1,0:T(8,128)(2,1)S(1)}, u32[]{:S(2)}, u32[]{:S(2)}) collective-permute-start(bf16[512,2048]{1,0:T(8,128)(2,1)S(1)} %get-tuple-element.86), channel_id=1, source_target_pairs={{0,1},{1,0},{2,3},{3,2},{4,5},{5,4},{6,7},{7,6},{8,9},{9,8},{10,11... | collective-permute-start | bytes 6291464 | tf_op jit(solution)/shard_map/ppermute | solution.py:340
  801.7 6.4 copy-start.35
  801.7 332.9 %reduce-scatter.10.cloned.1.call-start = ((), (), s32[]{:S(2)}) async-start(), calls=%async_computation.10 | async-start | bytes 4718592 | tf_op jit(solution)/shard_map/reduce_scatter | solution.py:423
  802.9 5.3 copy-start.7
  813.2 325.7 %reduce-scatter.14.cloned.1.call-start = ((), (), s32[]{:S(2)}) async-start(), calls=%async_computation.12 | async-start | bytes 9437184 | tf_op jit(solution)/shard_map/reduce_scatter | solution.py:414
  837.3 345.0 %reduce-scatter.6.cloned.1.call-start = ((), (), s32[]{:S(2)}) async-start(), calls=%async_computation.8 | async-start | bytes 7077888 | tf_op jit(solution)/shard_map/reduce_scatter | solution.py:432
  884.2 302.1 %reduce-scatter.12.cloned.1.call-start = ((), (), s32[]{:S(2)}) async-start(), calls=%async_computation.11 | async-start | bytes 18874368 | tf_op jit(solution)/shard_map/reduce_scatter | solution.py:411
  927.4 46.0 %copy-start.9 = (bf16[512,2048]{1,0:T(8,128)(2,1)S(1)}, bf16[512,2048]{1,0:T(8,128)(2,1)}, u32[]{:S(2)}) copy-start(bf16[512,2048]{1,0:T(8,128)(2,1)} %get-tuple-element.49) | copy-start | bytes 6291460
  927.4 45.9 %collective-permute-start.9 = (bf16[512,2048]{1,0:T(8,128)(2,1)}, bf16[512,2048]{1,0:T(8,128)(2,1)}, u32[]{:S(2)}, u32[]{:S(2)}) collective-permute-start(bf16[512,2048]{1,0:T(8,128)(2,1)} %get-tuple-element.50), channel_id=1, source_target_pairs={{0,1},{1,2},{2,3},{3,0},{4,5},{5,6},{6,7},{7,4},{8,9},{9,10},{10,1... | collective-permute-start | bytes 6291464 | tf_op jit(solution)/shard_map/ppermute | solution.py:404
  977.0 50.6 %collective-permute-start.10 = (bf16[512,2048]{1,0:T(8,128)(2,1)}, bf16[512,2048]{1,0:T(8,128)(2,1)}, u32[]{:S(2)}, u32[]{:S(2)}) collective-permute-start(bf16[512,2048]{1,0:T(8,128)(2,1)} %add_convert_fusion.5), channel_id=1, source_target_pairs={{0,1},{1,2},{2,3},{3,0},{4,5},{5,6},{6,7},{7,4},{8,9},{9,10},{10,1... | collective-permute-start | bytes 6291464 | tf_op jit(solution)/shard_map/ppermute | solution.py:404
  977.0 6.2 copy-start.36
  983.2 44.4 %copy-start.8 = (bf16[512,2048]{1,0:T(8,128)(2,1)S(1)}, bf16[512,2048]{1,0:T(8,128)(2,1)}, u32[]{:S(2)}) copy-start(bf16[512,2048]{1,0:T(8,128)(2,1)} %get-tuple-element.48) | copy-start | bytes 6291460
  991.1 81.5 %collective-permute-start.16 = (bf16[512,2048]{1,0:T(8,128)(2,1)}, bf16[512,2048]{1,0:T(8,128)(2,1)}, u32[]{:S(2)}, u32[]{:S(2)}) collective-permute-start(bf16[512,2048]{1,0:T(8,128)(2,1)} %add_convert_fusion), channel_id=1, source_target_pairs={{0,1},{1,0},{2,3},{3,2},{4,5},{5,4},{6,7},{7,6},{8,9},{9,8},{10,11... | collective-permute-start | bytes 6291464 | tf_op jit(solution)/shard_map/ppermute | solution.py:351
  991.1 3.7 collective-permute-start.24
  994.8 3.7 collective-permute-start.25
  998.5 33.0 %collective-permute-start.26 = (f32[256]{0:T(256)S(1)}, f32[256]{0:T(256)S(1)}, u32[]{:S(2)}, u32[]{:S(2)}) collective-permute-start(f32[256]{0:T(256)S(1)} %bitcast.90), channel_id=1, source_target_pairs={{0,4},{4,0},{8,12},{12,8},{16,20},{20,16},{24,28},{28,24},{1,5},{5... | collective-permute-start | bytes 3080 | tf_op jit(solution)/shard_map/ppermute | solution.py:316
  1031.5 91.7 %collective-permute-start.11 = (bf16[512,2048]{1,0:T(8,128)(2,1)}, bf16[512,2048]{1,0:T(8,128)(2,1)}, u32[]{:S(2)}, u32[]{:S(2)}) collective-permute-start(bf16[512,2048]{1,0:T(8,128)(2,1)} %add_convert_fusion.4), channel_id=1, source_target_pairs={{0,1},{1,2},{2,3},{3,0},{4,5},{5,6},{6,7},{7,4},{8,9},{9,10},{10,1... | collective-permute-start | bytes 6291464 | tf_op jit(solution)/shard_map/ppermute | solution.py:404
  1031.5 41.1 %slice-start = ((s8[8388608]{0:T(1024)(128)(4,1)}), s8[4194304]{0:T(1024)(128)(4,1)S(1)}, s32[]{:S(2)}) async-start(s8[8388608]{0:T(1024)(128)(4,1)} %bitcast.71), calls=%async_computation.13 | async-start | bytes 8388608
  1031.5 41.1 %copy-start.3 = (bf16[512,2048]{1,0:T(8,128)(2,1)S(1)}, bf16[512,2048]{1,0:T(8,128)(2,1)}, u32[]{:S(2)}) copy-start(bf16[512,2048]{1,0:T(8,128)(2,1)} %param.11) | copy-start | bytes 6291460
  1031.5 41.1 %slice-start.1 = ((s8[8388608]{0:T(1024)(128)(4,1)}), s8[4194304]{0:T(1024)(128)(4,1)S(1)}, s32[]{:S(2)}) async-start(s8[8388608]{0:T(1024)(128)(4,1)} %bitcast.71), calls=%async_computation.14 | async-start | bytes 8388608
  1031.5 41.1 %copy-start.21 = (f32[1,2048]{1,0:T(1,128)S(1)}, f32[1,2048]{1,0:T(1,128)}, u32[]{:S(2)}) copy-start(f32[1,2048]{1,0:T(1,128)} %copy-done.20) | copy-start | bytes 24580
  1031.5 41.1 %copy-start.29 = (f32[512]{0:T(512)S(1)}, f32[512]{0:T(512)}, u32[]{:S(2)}) copy-start(f32[512]{0:T(512)} %copy-done.28) | copy-start | bytes 6148
  1031.5 41.1 %copy-start.37 = (bf16[1024,1536]{1,0:T(8,128)(2,1)S(1)}, bf16[1024,1536]{1,0:T(8,128)(2,1)}, u32[]{:S(2)}) copy-start(bf16[1024,1536]{1,0:T(8,128)(2,1)} %attend_back.2) | copy-start | bytes 9437188
  1031.6 76.4 %collective-permute-start.27 = (f32[128]{0:T(128)S(1)}, f32[128]{0:T(128)S(1)}, u32[]{:S(2)}, u32[]{:S(2)}) collective-permute-start(f32[128]{0:T(128)S(1)} %fusion.64), channel_id=1, source_target_pairs={{0,2},{1,3},{2,0},{3,1},{4,6},{5,7},{6,4},{7,5},{8,10},{9,11},{10,... | collective-permute-start | bytes 1544 | tf_op jit(solution)/shard_map/ppermute | solution.py:316
  1037.7 79.7 %copy-start.31 = (f32[512]{0:T(512)S(1)}, f32[512]{0:T(512)}, u32[]{:S(2)}) copy-start(f32[512]{0:T(512)} %copy-done.30) | copy-start | bytes 6148
  1037.7 85.4 %copy-start.19 = (f32[1,2048]{1,0:T(1,128)S(1)}, f32[1,2048]{1,0:T(1,128)}, u32[]{:S(2)}) copy-start(f32[1,2048]{1,0:T(1,128)} %copy-done.18) | copy-start | bytes 24580
  1037.7 85.4 %copy-start.23 = (f32[512]{0:T(512)S(1)}, f32[512]{0:T(512)}, u32[]{:S(2)}) copy-start(f32[512]{0:T(512)} %copy-done.22) | copy-start | bytes 6148
  1037.7 85.4 %copy-start.27 = (f32[512]{0:T(512)S(1)}, f32[512]{0:T(512)}, u32[]{:S(2)}) copy-start(f32[512]{0:T(512)} %copy-done.26) | copy-start | bytes 6148
  1080.2 27.9 %collective-permute-start.19 = (f32[1024]{0:T(1024)S(1)}, f32[1024]{0:T(1024)S(1)}, u32[]{:S(2)}, u32[]{:S(2)}) collective-permute-start(f32[1024]{0:T(1024)S(1)} %bitcast.85), channel_id=1, source_target_pairs={{0,16},{4,20},{8,24},{12,28},{16,0},{20,4},{24,8},{28,12},{1,17},{... | collective-permute-start | bytes 12296 | tf_op jit(solution)/shard_map/ppermute | solution.py:316
  1108.1 6.3 collective-permute-start.20
  1109.9 6.0 collective-permute-start.28
  1114.4 2.0 collective-permute-start.21
  1116.5 4.5 collective-permute-start.22
  1121.1 13.0 %collective-permute-start.23 = (f32[64]{0:T(128)S(1)}, f32[64]{0:T(128)S(1)}, u32[]{:S(2)}, u32[]{:S(2)}) collective-permute-start(f32[64]{0:T(128)S(1)} %fusion.61), channel_id=1, source_target_pairs={{0,1},{1,0},{2,3},{3,2},{4,5},{5,4},{6,7},{7,6},{8,9},{9,8},{10,11... | collective-permute-start | bytes 776 | tf_op jit(solution)/shard_map/ppermute | solution.py:316
  1133.8 48.5 %collective-permute-start.17 = (bf16[256,1536]{1,0:T(8,128)(2,1)}, bf16[256,1536]{1,0:T(8,128)(2,1)S(1)}, u32[]{:S(2)}, u32[]{:S(2)}) collective-permute-start(bf16[256,1536]{1,0:T(8,128)(2,1)} %reduce-scatter.8.cloned.1.call-done), channel_id=1, source_target_pairs={{0,2},{1,3},{2,0},{3,1},{4,6},{5,7},{6,4},{7,5},{8,10},{9,11},{10,... | collective-permute-start | bytes 2359304 | tf_op jit(solution)/shard_map/ppermute | solution.py:333
  1136.2 44.2 %copy-start.17 = (bf16[256,1024]{0,1:T(8,128)(2,1)S(1)}, bf16[256,1024]{0,1:T(8,128)(2,1)}, u32[]{:S(2)}) copy-start(bf16[256,1024]{0,1:T(8,128)(2,1)} %reduce-scatter.10.cloned.1.call-done) | copy-start | bytes 1572868
  1136.2 44.2 %collective-permute-start.18 = (bf16[256,512]{0,1:T(8,128)(2,1)}, bf16[256,512]{0,1:T(8,128)(2,1)}, u32[]{:S(2)}, u32[]{:S(2)}) collective-permute-start(bf16[256,512]{0,1:T(8,128)(2,1)} %slice.315), channel_id=1, source_target_pairs={{0,2},{1,3},{2,0},{3,1},{4,6},{5,7},{6,4},{7,5},{8,10},{9,11},{10,... | collective-permute-start | bytes 786440 | tf_op jit(solution)/shard_map/ppermute | solution.py:333
  (14 other events, 27.0 us)
Sparse Core Ops, SparseCore 0:
  19.9 56.9 all-gather.3
  79.4 54.2 all-gather.5
  135.6 125.1 all-gather.7
  801.8 59.1 reduce-scatter.7
  864.1 51.0 reduce-scatter.9
  918.5 71.5 reduce-scatter.13
  993.5 61.7 reduce-scatter.5
  1058.8 116.2 reduce-scatter.11
